TPU v7x, 32 devices: a whole 2x2x4 slice. The times are simulated.
32 devices in a mesh: rows: 8 (over z, y), cols: 4 (over x, core).
Axes of the slice: x: 2, y: 2, z: 4, core: 2. Of those that a mesh axis runs over, the one named last changes fastest.
Arguments:
- genotypes: int32 [5120, 2048], P('rows', 'cols'), may hold values from 0 to 2
- frequencies: float32 [2048], P('cols'), may hold values from 0.05 to 0.5
- traits: bfloat16 [5120, 32768], P('rows', 'cols'), may hold values from -6 to 6
- geno_sketch: bfloat16 [2048, 512], P('cols'), may hold values from -0.125 to 0.125
- trait_sketch: bfloat16 [32768, 512], P('cols'), may hold values from -0.03125 to 0.03125
- initial: float32 [512, 256], replicated, may hold values from -6 to 6
Outputs:
- geno_scores: bfloat16 [5120, 256], P('rows')
- trait_scores: bfloat16 [5120, 256], P('rows')
- geno_loadings: float32 [256, 2048], P('rows', 'cols')
- trait_loadings: float32 [256, 32768], P('rows', 'cols')
All inputs are finite; a program needn't handle non-finite values.
Results may differ from a plain program's by a relative error of at most 0.0059.
Values sent between devices are 32-bit elements; how exact they have to be, the bound alone decides.
No kernel may reach another device: no remote copies, remote signals or barrier semaphores. Data moves between devices by JAX's collectives and lax.ppermute only.
A program may use at most 128 MiB of HBM per device.

v0:
```python
import functools
import math

import jax
import jax.numpy as jnp
from jax import lax
from jax.experimental import pallas as pl
from jax.experimental.pallas import tpu as pltpu
from jax.sharding import PartitionSpec as P

EXACT = lax.Precision.HIGHEST
CLOSE = lax.Precision.HIGH


def eliminate(block, out_ref, tall=8):
    size = block.shape[0]
    shape = (8, size)
    lanes = lax.broadcasted_iota(jnp.int32, shape, 1)
    subs = lax.broadcasted_iota(jnp.int32, shape, 0)
    groups = [block[8 * g : 8 * g + 8, :] for g in range(size // 8)]
    for first in range(0, size, tall):
        own, s = divmod(first, 8)
        here = groups[own]
        spread = [jnp.broadcast_to(here[:, first + k : first + k + 1], shape) for k in range(tall)]
        a = [[jnp.broadcast_to(spread[k][s + i : s + i + 1, :], shape) for k in range(i + 1)] for i in range(tall)]
        inside = (lanes >= first) & (lanes < first + tall)
        unit = jnp.where(inside, jnp.where(lanes - first == subs - s, 1.0, 0.0), here)
        rows = [jnp.broadcast_to(unit[s + k : s + k + 1, :], shape) for k in range(tall)]
        inverse, lower = [], {}
        for i in range(tall):
            inverse.append(1.0 / a[i][i])
            for k in range(i + 1, tall):
                lower[k, i] = a[k][i] * inverse[i]
                for m in range(i + 1, k + 1):
                    a[k][m] = a[k][m] - lower[k, i] * a[m][i]
                rows[k] = rows[k] - lower[k, i] * rows[i]
        final = rows[0] * lax.rsqrt(a[0][0])
        for i in range(1, tall):
            final = jnp.where(subs == s + i, rows[i] * lax.rsqrt(a[i][i]), final)
        out_ref[first : first + tall, :] = jnp.where(lanes <= 8 * own + subs, final, 0.0)[s : s + tall, :]
        back = [None] * tall
        for k in reversed(range(tall)):
            back[k] = rows[k] * inverse[k]
            for i in range(k + 1, tall):
                back[k] = back[k] - lower[i, k] * back[i]
        for g in range(own if s + tall < 8 else own + 1, size // 8):
            old = groups[g]
            fresh = jnp.where(inside, 0.0, old)
            for k in range(tall):
                col = spread[k] if g == own else jnp.broadcast_to(old[:, first + k : first + k + 1], shape)
                fresh = fresh - col * back[k]
            groups[g] = fresh if g > own else jnp.where(subs >= s + tall, fresh, old)


def factor_in_place(ref, small_ref):
    n, width = ref.shape[0], small_ref.shape[0]
    wide = lax.broadcasted_iota(jnp.int32, (width, n), 1)
    deep = lax.broadcasted_iota(jnp.int32, (width, n), 0)

    def step(k, carry):
        at = pl.multiple_of(k * width, width)
        eliminate(ref[pl.ds(at, width), pl.ds(at, width)], small_ref)
        panel = ref[pl.ds(at, width), :]
        inside = (wide >= at) & (wide < at + width)
        panel = jnp.where(inside, jnp.where(wide - at == deep, 1.0, 0.0), panel)
        panel = jnp.dot(small_ref[...], panel, precision=EXACT, preferred_element_type=jnp.float32)
        below = jnp.where(wide >= at + width, panel, 0.0)
        update = lax.dot_general(
            below, panel, (((0,), (0,)), ((), ())), precision=EXACT, preferred_element_type=jnp.float32
        )
        for i in range(n // width):
            old = ref[i * width : (i + 1) * width, :]
            old = jnp.where(inside & (i > k), 0.0, old)
            ref[i * width : (i + 1) * width, :] = old - update[i * width : (i + 1) * width, :]
        ref[pl.ds(at, width), :] = jnp.where(wide < at + width, panel, 0.0)
        return carry

    lax.fori_loop(0, n // width, step, 0)


def factor_whole_kernel(gram_ref, inverse_ref, small_ref, *, scale):
    inverse_ref[...] = gram_ref[...] * scale
    factor_in_place(inverse_ref, small_ref)


def factor_pieces_kernel(place_ref, *refs, scale):
    piece_refs, (inverse_ref, small_ref, held_ref) = refs[:4], refs[4:]
    half = inverse_ref.shape[0] // 2
    rows = half // 2
    for at, piece_ref in enumerate(piece_refs):
        chip, side = place_ref[0] ^ (at // 2), place_ref[1] ^ (at % 2)
        held_ref[chip, pl.ds(pl.multiple_of(side * rows, rows), rows), :] = piece_ref[...] * scale
    inverse_ref[:half, :half] = held_ref[0, :, :half]
    inverse_ref[:half, half : half + rows] = held_ref[0, :, half:]
    inverse_ref[:half, half + rows :] = held_ref[1, :, half:]
    inverse_ref[half:, :half] = jnp.zeros((half, half), jnp.float32)
    inverse_ref[half:, half:] = held_ref[1, :, :half]
    factor_in_place(inverse_ref, small_ref)


def inverse_factor(pieces, place, size, scale):
    width = math.gcd(size, 128)
    vmem = pl.BlockSpec(memory_space=pltpu.VMEM)
    scratch = [pltpu.VMEM((width, width), jnp.float32)]
    if place is None:
        kernel, specs = factor_whole_kernel, [vmem]
    else:
        kernel, specs = factor_pieces_kernel, [pl.BlockSpec(memory_space=pltpu.SMEM)] + [vmem] * 4
        scratch.append(pltpu.VMEM((2, size // 2, size // 4 * 3), jnp.float32))
        pieces = (place, *pieces)
    return pl.pallas_call(
        functools.partial(kernel, scale=scale),
        out_shape=jax.ShapeDtypeStruct((size, size), jnp.float32),
        in_specs=specs,
        out_specs=vmem,
        scratch_shapes=scratch,
        name="inverse_factor",
    )(*pieces)


def standard(genotypes, frequencies):
    spread = lax.rsqrt(2.0 * frequencies * (1.0 - frequencies))
    return ((genotypes.astype(jnp.float32) - 2.0 * frequencies) * spread).astype(jnp.bfloat16)


def unit_columns(matrix):
    return matrix * lax.rsqrt(jnp.mean(matrix * matrix, axis=0, keepdims=True) + 1e-06)


def dot(left_side, right_side, contract, precision):
    return lax.dot_general(
        left_side,
        right_side,
        ((contract[:1], contract[1:]), ((), ())),
        precision=precision,
        preferred_element_type=jnp.float32,
    )


def masks_of(size):
    return [1 << bit for bit in range(size.bit_length() - 1)]


def swap(value, axis, mask):
    size = lax.axis_size(axis)
    return lax.ppermute(value, axis, [(i, i ^ mask) for i in range(size)])


def side_of(axis, mask):
    return jnp.minimum(lax.axis_index(axis) & mask, 1)


def halve(value, axis, mask):
    half = value.shape[0] // 2
    side = side_of(axis, mask)
    kept = lax.dynamic_slice_in_dim(value, side * half, half)
    sent = lax.dynamic_slice_in_dim(value, (1 - side) * half, half)
    return kept + swap(sent, axis, mask)


def double(value, axis, mask):
    side = side_of(axis, mask)
    half = value.shape[0]
    whole = jnp.concatenate([value, value], axis=0)
    return lax.dynamic_update_slice_in_dim(whole, swap(value, axis, mask), (1 - side) * half, 0)


def ring_place(index, size):
    return jnp.where(index % 2 == 0, index // 2, size - (index + 1) // 2)


def ring_member(place, size):
    return jnp.where(2 * place < size, 2 * place, 2 * (size - place) - 1)


def ring_scatter(take, size, forward):
    members = [2 * q if 2 * q < size else 2 * (size - q) - 1 for q in range(size)]
    pairs = [(members[q], members[(q + 1) % size]) for q in range(size)]
    if not forward:
        pairs = [(b, a) for a, b in pairs]
    turn = 1 if forward else -1
    place = ring_place(lax.axis_index("rows"), size)
    total = take(ring_member((place - turn + size) % size, size))
    for step in range(size - 1):
        arrived = lax.ppermute(total, "rows", pairs)
        total = arrived + take(ring_member((place - turn * (step + 2) + 2 * size) % size, size))
    return total


def sum_rows(value, masks):
    for mask in masks[:-1]:
        value = halve(value, "rows", mask)
    value = value + swap(value, "rows", masks[-1])
    for mask in reversed(masks[1:-1]):
        value = double(value, "rows", mask)
    return value


def on_device(genotypes, frequencies, traits, geno_sketch, trait_sketch, initial):
    row_count, col_count = lax.axis_size("rows"), lax.axis_size("cols")
    people = genotypes.shape[0] * row_count
    size = geno_sketch.shape[1]
    col = lax.axis_index("cols")
    core, chip = col % 2, col // 2
    chips = col_count // 2
    wide_masks = masks_of(col_count)[1:]
    row_masks = masks_of(row_count)

    standardized = standard(genotypes, frequencies)

    def over_chips(part):
        for mask in wide_masks:
            moved = swap(part, "cols", mask)
            part = part + moved
        return part

    partial_geno = jnp.dot(standardized, geno_sketch, preferred_element_type=jnp.float32)
    chip_geno = halve(partial_geno, "cols", 1)
    height = genotypes.shape[0] // 2
    late_traits, chip_geno = lax.optimization_barrier((traits, chip_geno))
    partial_trait = jnp.dot(late_traits, trait_sketch, preferred_element_type=jnp.float32)
    half_geno = over_chips(chip_geno)
    half_trait = over_chips(halve(partial_trait, "cols", 1))

    mine = jnp.where(core == 0, half_geno, half_trait)
    others = jnp.where(core == 0, half_trait, half_geno)
    arrived = swap(others, "cols", 1)

    def gram_of(left_of, right_of):
        return sum(dot(left_of(view), right_of(view), (0, 0), EXACT) for view in (mine, arrived))

    def columns(at, width):
        return lambda view: lax.dynamic_slice_in_dim(view, at, width, 1)

    if chips == 2:
        half, quarter = size // 2, size // 4
        block = gram_of(columns(chip * half, half), columns(chip * half, half))
        side = gram_of(columns(0, half), columns(half + chip * quarter, quarter))
        gram = jnp.concatenate([block, side], axis=1)
    else:
        strip = size // chips
        gram = gram_of(columns(chip * strip, strip), lambda view: view)
    mine, others, arrived, gram = lax.optimization_barrier((mine, others, arrived, gram))
    gram = sum_rows(gram, row_masks)

    whole_mine = jnp.concatenate([mine, mine], axis=0)
    own = lax.dynamic_update_slice_in_dim(whole_mine, arrived, (1 - core) * height, 0)
    whole_others = jnp.concatenate([others, others], axis=0)
    other = lax.dynamic_update_slice_in_dim(whole_others, swap(mine, "cols", 1), (1 - core) * height, 0)
    sketch_geno = jnp.where(core == 0, own, other)
    sketch_trait = jnp.where(core == 0, other, own)

    strip = size // col_count
    cross_strip = lax.dynamic_slice_in_dim(sketch_geno, (core * chips + chip) * strip, strip, 1)
    cross = sum_rows(dot(cross_strip, sketch_trait, (0, 0), EXACT), row_masks)
    cross = double(cross, "rows", row_masks[0])
    for mask in wide_masks:
        cross = double(cross, "cols", mask)

    if chips == 2:
        beside = swap(gram, "rows", 1)
        across = swap(gram, "cols", 2)
        cells = [(r, c) for r in range(row_count) for c in range(col_count)]
        flat = [(r * col_count + c, (r ^ 1) * col_count + (c ^ 2)) for r, c in cells]
        corner = lax.ppermute(gram, ("rows", "cols"), flat)
        place = jnp.stack([chip, side_of("rows", 1)])
        own_inverse = inverse_factor((gram, beside, across, corner), place, size, 1.0 / people)
    else:
        gram = double(gram, "rows", row_masks[0])
        for mask in wide_masks:
            gram = double(gram, "cols", mask)
        own_inverse = inverse_factor((gram,), None, size, 1.0 / people)
    cross = double(cross, "cols", 1)
    other_inverse = swap(own_inverse, "cols", 1)
    inverse_geno = jnp.where(core == 0, own_inverse, other_inverse)
    inverse_trait = jnp.where(core == 0, other_inverse, own_inverse)

    moved = dot(cross, dot(inverse_trait, initial, (0, 0), CLOSE), (1, 0), CLOSE) / people
    left_dirs = unit_columns(dot(inverse_geno, moved, (1, 0), CLOSE))
    geno_weights = dot(inverse_geno, left_dirs, (0, 0), CLOSE)
    moved = dot(cross, geno_weights, (0, 0), CLOSE) / people
    right_dirs = unit_columns(dot(inverse_trait, moved, (1, 0), CLOSE))
    trait_weights = dot(inverse_trait, right_dirs, (0, 0), CLOSE)

    root_size = math.sqrt(size)
    geno_scores = (dot(sketch_geno, geno_weights, (1, 0), CLOSE) / root_size).astype(jnp.bfloat16)
    trait_scores = (dot(sketch_trait, trait_weights, (1, 0), CLOSE) / root_size).astype(jnp.bfloat16)

    def term(scores, block):
        return lax.dot_general(scores, block, (((0,), (0,)), ((), ())), preferred_element_type=jnp.float32)

    pairs = geno_scores.shape[1]
    share = pairs // row_count
    streams = 4
    geno_share, trait_share = standardized.shape[1] // streams, traits.shape[1] // streams
    geno_term = term(geno_scores, standardized)
    summed = []
    for at in range(streams):
        trait_term = term(trait_scores, traits[:, at * trait_share : (at + 1) * trait_share])
        geno_piece = geno_term[:, at * geno_share : (at + 1) * geno_share]

        def take(member, geno_piece=geno_piece, trait_term=trait_term):
            return jnp.concatenate(
                [lax.dynamic_slice_in_dim(piece, member * share, share) for piece in (geno_piece, trait_term)],
                axis=1,
            )

        summed.append(ring_scatter(take, row_count, at % 2 == 0))
    root_people = math.sqrt(people)
    geno_loadings = jnp.concatenate([piece[:, :geno_share] for piece in summed], axis=1) / root_people
    trait_loadings = jnp.concatenate([piece[:, geno_share:] for piece in summed], axis=1) / root_people
    return (geno_scores, trait_scores, geno_loadings, trait_loadings)


def solution(mesh):
    placed = (
        P("rows", "cols"),
        P("cols"),
        P("rows", "cols"),
        P("cols", None),
        P("cols", None),
        P(),
    )
    return jax.shard_map(
        on_device,
        mesh=mesh,
        in_specs=placed,
        out_specs=(P("rows", None), P("rows", None), P("rows", "cols"), P("rows", "cols")),
        check_vma=False,
    )
```

profile of v0, /device:TPU:0, one launch (start us, length us, event | category | flops | bytes accessed | tf_op | source)
XLA Modules:
  0.0 245.7 jit_solution(3381534747285243786)
XLA Ops:
  6.0 10.7 %fusion.35 = f32[640,512]{1,0:T(8,128)S(1)} fusion(bf16[640,8192]{1,0:T(8,128)(2,1)} %param.8, bf16[8192,512]{1,0:T(8,128)(2,1)} %param.10), kind=kOutput, calls=%fused_computation.180 | convolution fusion | flops 5368709120 | bytes 20185088 | tf_op jit(solution)/shard_map/dot_general | solution.py:221
  21.9 13.4 %collective-permute-done.1 = f32[320,512]{1,0:T(8,128)S(1)} collective-permute-done((f32[320,512]{1,0:T(8,128)S(1)}, f32[320,512]{1,0:T(8,128)S(1)}, u32[]{:S(2)}, u32[]{:S(2)}) %collective-permute-start.1) | collective-permute-done | bytes 655392 | tf_op jit(solution)/shard_map/ppermute | solution.py:146
  36.2 12.9 %collective-permute-done.3 = f32[320,512]{1,0:T(8,128)S(1)} collective-permute-done((f32[320,512]{1,0:T(8,128)S(1)}, f32[320,512]{1,0:T(8,128)S(1)}, u32[]{:S(2)}, u32[]{:S(2)}) %collective-permute-start.3) | collective-permute-done | bytes 655392 | tf_op jit(solution)/shard_map/ppermute | solution.py:146
  59.7 3.6 %collective-permute-done.6 = f32[128,384]{1,0:T(8,128)} collective-permute-done((f32[128,384]{1,0:T(8,128)S(1)}, f32[128,384]{1,0:T(8,128)}, u32[]{:S(2)}, u32[]{:S(2)}) %collective-permute-start.6) | collective-permute-done | bytes 196640 | tf_op jit(solution)/shard_map/ppermute | solution.py:146
  66.2 2.8 %collective-permute-done.7 = f32[64,384]{1,0:T(8,128)S(1)} collective-permute-done((f32[64,384]{1,0:T(8,128)S(1)}, f32[64,384]{1,0:T(8,128)S(1)}, u32[]{:S(2)}, u32[]{:S(2)}) %collective-permute-start.7) | collective-permute-done | bytes 98336 | tf_op jit(solution)/shard_map/ppermute | solution.py:146
  69.0 2.9 %collective-permute-start.8 = (f32[64,384]{1,0:T(8,128)S(1)}, f32[64,384]{1,0:T(8,128)}, u32[]{:S(2)}, u32[]{:S(2)}) collective-permute-start(f32[64,384]{1,0:T(8,128)S(1)} %dynamic-slice_add_fusion.4), channel_id=1, source_target_pairs={{0,16},{4,20},{8,24},{12,28},{16,0},{20,4},{24,8},{28,12},{1,17},{... | collective-permute-start | bytes 294920 | tf_op jit(solution)/shard_map/ppermute | solution.py:146
  91.2 33.0 %inverse_factor.1 = f32[512,512]{1,0:T(8,128)} custom-call(s32[2]{0:T(128)} %pad_add_fusion.place_ref, f32[128,384]{1,0:T(8,128)} %copy-done.14, f32[128,384]{1,0:T(8,128)} %copy-done.17, f32[128,384]{1,0:T(8,128)} %copy-done.18, f32[128,384]{1,0:T(8,128)} %copy-done.19), custom_call_target="tpu_custom_call" | custom-call | tf_op jit(solution)/shard_map/inverse_factor/pallas_call | solution.py:111
  125.8 3.0 %collective-permute-done.17 = f32[32,512]{1,0:T(8,128)S(1)} collective-permute-done((f32[32,512]{1,0:T(8,128)S(1)}, f32[32,512]{1,0:T(8,128)S(1)}, u32[]{:S(2)}, u32[]{:S(2)}) %collective-permute-start.17) | collective-permute-done | bytes 65568 | tf_op jit(solution)/shard_map/ppermute | solution.py:146
  130.1 3.8 %collective-permute-done.18 = f32[64,512]{1,0:T(8,128)S(1)} collective-permute-done((f32[64,512]{1,0:T(8,128)S(1)}, f32[64,512]{1,0:T(8,128)S(1)}, u32[]{:S(2)}, u32[]{:S(2)}) %collective-permute-start.18) | collective-permute-done | bytes 131104 | tf_op jit(solution)/shard_map/ppermute | solution.py:146
  135.4 5.5 %collective-permute-done.19 = f32[128,512]{1,0:T(8,128)S(1)} collective-permute-done((f32[128,512]{1,0:T(8,128)S(1)}, f32[128,512]{1,0:T(8,128)S(1)}, u32[]{:S(2)}, u32[]{:S(2)}) %collective-permute-start.19) | collective-permute-done | bytes 262176 | tf_op jit(solution)/shard_map/ppermute | solution.py:146
  161.2 3.1 %collective-permute-done.42 = f32[32,2176]{1,0:T(8,128)S(1)} collective-permute-done((f32[32,2176]{1,0:T(8,128)S(1)}, f32[32,2176]{1,0:T(8,128)S(1)}, u32[]{:S(2)}, u32[]{:S(2)}) %collective-permute-start.42) | collective-permute-done | bytes 278560 | tf_op jit(solution)/shard_map/ppermute | solution.py:185
  167.2 3.1 %collective-permute-done.28 = f32[32,2176]{1,0:T(8,128)S(1)} collective-permute-done((f32[32,2176]{1,0:T(8,128)S(1)}, f32[32,2176]{1,0:T(8,128)S(1)}, u32[]{:S(2)}, u32[]{:S(2)}) %collective-permute-start.28) | collective-permute-done | bytes 278560 | tf_op jit(solution)/shard_map/ppermute | solution.py:185
  173.2 3.1 %collective-permute-done.43 = f32[32,2176]{1,0:T(8,128)S(1)} collective-permute-done((f32[32,2176]{1,0:T(8,128)S(1)}, f32[32,2176]{1,0:T(8,128)S(1)}, u32[]{:S(2)}, u32[]{:S(2)}) %collective-permute-start.43) | collective-permute-done | bytes 278560 | tf_op jit(solution)/shard_map/ppermute | solution.py:185
  179.1 3.1 %collective-permute-done.29 = f32[32,2176]{1,0:T(8,128)S(1)} collective-permute-done((f32[32,2176]{1,0:T(8,128)S(1)}, f32[32,2176]{1,0:T(8,128)S(1)}, u32[]{:S(2)}, u32[]{:S(2)}) %collective-permute-start.29) | collective-permute-done | bytes 278560 | tf_op jit(solution)/shard_map/ppermute | solution.py:185
  185.1 3.1 %collective-permute-done.44 = f32[32,2176]{1,0:T(8,128)S(1)} collective-permute-done((f32[32,2176]{1,0:T(8,128)S(1)}, f32[32,2176]{1,0:T(8,128)S(1)}, u32[]{:S(2)}, u32[]{:S(2)}) %collective-permute-start.44) | collective-permute-done | bytes 278560 | tf_op jit(solution)/shard_map/ppermute | solution.py:185
  191.1 3.1 %collective-permute-done.30 = f32[32,2176]{1,0:T(8,128)S(1)} collective-permute-done((f32[32,2176]{1,0:T(8,128)S(1)}, f32[32,2176]{1,0:T(8,128)S(1)}, u32[]{:S(2)}, u32[]{:S(2)}) %collective-permute-start.30) | collective-permute-done | bytes 278560 | tf_op jit(solution)/shard_map/ppermute | solution.py:185
  197.1 3.1 %collective-permute-done.45 = f32[32,2176]{1,0:T(8,128)S(1)} collective-permute-done((f32[32,2176]{1,0:T(8,128)S(1)}, f32[32,2176]{1,0:T(8,128)S(1)}, u32[]{:S(2)}, u32[]{:S(2)}) %collective-permute-start.45) | collective-permute-done | bytes 278560 | tf_op jit(solution)/shard_map/ppermute | solution.py:185
  203.0 3.1 %collective-permute-done.31 = f32[32,2176]{1,0:T(8,128)S(1)} collective-permute-done((f32[32,2176]{1,0:T(8,128)S(1)}, f32[32,2176]{1,0:T(8,128)S(1)}, u32[]{:S(2)}, u32[]{:S(2)}) %collective-permute-start.31) | collective-permute-done | bytes 278560 | tf_op jit(solution)/shard_map/ppermute | solution.py:185
  209.0 3.1 %collective-permute-done.46 = f32[32,2176]{1,0:T(8,128)S(1)} collective-permute-done((f32[32,2176]{1,0:T(8,128)S(1)}, f32[32,2176]{1,0:T(8,128)S(1)}, u32[]{:S(2)}, u32[]{:S(2)}) %collective-permute-start.46) | collective-permute-done | bytes 278560 | tf_op jit(solution)/shard_map/ppermute | solution.py:185
  215.0 3.1 %collective-permute-done.32 = f32[32,2176]{1,0:T(8,128)S(1)} collective-permute-done((f32[32,2176]{1,0:T(8,128)S(1)}, f32[32,2176]{1,0:T(8,128)S(1)}, u32[]{:S(2)}, u32[]{:S(2)}) %collective-permute-start.32) | collective-permute-done | bytes 278560 | tf_op jit(solution)/shard_map/ppermute | solution.py:185
  220.9 3.1 %collective-permute-done.47 = f32[32,2176]{1,0:T(8,128)S(1)} collective-permute-done((f32[32,2176]{1,0:T(8,128)S(1)}, f32[32,2176]{1,0:T(8,128)S(1)}, u32[]{:S(2)}, u32[]{:S(2)}) %collective-permute-start.47) | collective-permute-done | bytes 278560 | tf_op jit(solution)/shard_map/ppermute | solution.py:185
  226.9 3.1 %collective-permute-done.33 = f32[32,2176]{1,0:T(8,128)S(1)} collective-permute-done((f32[32,2176]{1,0:T(8,128)S(1)}, f32[32,2176]{1,0:T(8,128)S(1)}, u32[]{:S(2)}, u32[]{:S(2)}) %collective-permute-start.33) | collective-permute-done | bytes 278560 | tf_op jit(solution)/shard_map/ppermute | solution.py:185
  232.9 3.1 %collective-permute-done.48 = f32[32,2176]{1,0:T(8,128)S(1)} collective-permute-done((f32[32,2176]{1,0:T(8,128)S(1)}, f32[32,2176]{1,0:T(8,128)S(1)}, u32[]{:S(2)}, u32[]{:S(2)}) %collective-permute-start.48) | collective-permute-done | bytes 278560 | tf_op jit(solution)/shard_map/ppermute | solution.py:185
  238.0 3.9 %collective-permute-done.34 = f32[32,2176]{1,0:T(8,128)S(1)} collective-permute-done((f32[32,2176]{1,0:T(8,128)S(1)}, f32[32,2176]{1,0:T(8,128)S(1)}, u32[]{:S(2)}, u32[]{:S(2)}) %collective-permute-start.34) | collective-permute-done | bytes 278560 | tf_op jit(solution)/shard_map/ppermute | solution.py:185
  (231 shorter events, 108.8 us)
Async XLA Ops:
  17.2 18.2 %collective-permute-start.1 = (f32[320,512]{1,0:T(8,128)S(1)}, f32[320,512]{1,0:T(8,128)S(1)}, u32[]{:S(2)}, u32[]{:S(2)}) collective-permute-start(f32[320,512]{1,0:T(8,128)S(1)} %dynamic-slice_add_fusion.1), channel_id=1, source_target_pairs={{0,2},{1,3},{2,0},{3,1},{4,6},{5,7},{6,4},{7,5},{8,10},{9,11},{10,... | collective-permute-start | bytes 1966088 | tf_op jit(solution)/shard_map/ppermute | solution.py:146
  19.9 29.2 %collective-permute-start.3 = (f32[320,512]{1,0:T(8,128)S(1)}, f32[320,512]{1,0:T(8,128)S(1)}, u32[]{:S(2)}, u32[]{:S(2)}) collective-permute-start(f32[320,512]{1,0:T(8,128)S(1)} %dynamic-slice_add_fusion), channel_id=1, source_target_pairs={{0,2},{1,3},{2,0},{3,1},{4,6},{5,7},{6,4},{7,5},{8,10},{9,11},{10,... | collective-permute-start | bytes 1966088 | tf_op jit(solution)/shard_map/ppermute | solution.py:146
  58.0 13.9 %collective-permute-start.5 = (f32[320,512]{1,0:T(8,128)S(1)}, f32[320,512]{1,0:T(8,128)S(1)}, u32[]{:S(2)}, u32[]{:S(2)}) collective-permute-start(f32[320,512]{1,0:T(8,128)S(1)} %get-tuple-element.12), channel_id=1, source_target_pairs={{0,1},{1,0},{2,3},{3,2},{4,5},{5,4},{6,7},{7,6},{8,9},{9,8},{10,11... | collective-permute-start | bytes 1966088 | tf_op jit(solution)/shard_map/ppermute | solution.py:146
  84.7 39.5 %collective-permute-start.16 = (f32[32,512]{1,0:T(8,128)S(1)}, f32[32,512]{1,0:T(8,128)S(1)}, u32[]{:S(2)}, u32[]{:S(2)}) collective-permute-start(f32[32,512]{1,0:T(8,128)S(1)} %dynamic-slice_add_fusion.5), channel_id=1, source_target_pairs={{0,16},{4,20},{8,24},{12,28},{16,0},{20,4},{24,8},{28,12},{1,17},{... | collective-permute-start | bytes 196616 | tf_op jit(solution)/shard_map/ppermute | solution.py:146
  124.1 17.0 %collective-permute-start.13 = (f32[512,512]{1,0:T(8,128)}, f32[512,512]{1,0:T(8,128)}, u32[]{:S(2)}, u32[]{:S(2)}) collective-permute-start(f32[512,512]{1,0:T(8,128)} %inverse_factor.1), channel_id=1, source_target_pairs={{0,1},{1,0},{2,3},{3,2},{4,5},{5,4},{6,7},{7,6},{8,9},{9,8},{10,11... | collective-permute-start | bytes 3145736 | tf_op jit(solution)/shard_map/ppermute | solution.py:146
  160.2 12.1 %collective-permute-start.21 = (f32[32,2176]{1,0:T(8,128)S(1)}, f32[32,2176]{1,0:T(8,128)S(1)}, u32[]{:S(2)}, u32[]{:S(2)}) collective-permute-start(f32[32,2176]{1,0:T(8,128)S(1)} %pad_maximum_fusion.5), channel_id=1, source_target_pairs={{0,8},{8,16},{16,24},{24,28},{28,20},{20,12},{12,4},{4,0},{1,9},{9... | collective-permute-start | bytes 835592 | tf_op jit(solution)/shard_map/ppermute | solution.py:185
  164.3 11.9 %collective-permute-start.43 = (f32[32,2176]{1,0:T(8,128)S(1)}, f32[32,2176]{1,0:T(8,128)S(1)}, u32[]{:S(2)}, u32[]{:S(2)}) collective-permute-start(f32[32,2176]{1,0:T(8,128)S(1)} %maximum_add_fusion.21), channel_id=1, source_target_pairs={{8,0},{16,8},{24,16},{28,24},{20,28},{12,20},{4,12},{0,4},{9,1},{1... | collective-permute-start | bytes 835592 | tf_op jit(solution)/shard_map/ppermute | solution.py:185
  166.3 11.9 %collective-permute-start.36 = (f32[32,2176]{1,0:T(8,128)S(1)}, f32[32,2176]{1,0:T(8,128)S(1)}, u32[]{:S(2)}, u32[]{:S(2)}) collective-permute-start(f32[32,2176]{1,0:T(8,128)S(1)} %maximum_add_fusion.14), channel_id=1, source_target_pairs={{0,8},{8,16},{16,24},{24,28},{28,20},{20,12},{12,4},{4,0},{1,9},{9... | collective-permute-start | bytes 835592 | tf_op jit(solution)/shard_map/ppermute | solution.py:185
  170.3 11.9 %collective-permute-start.29 = (f32[32,2176]{1,0:T(8,128)S(1)}, f32[32,2176]{1,0:T(8,128)S(1)}, u32[]{:S(2)}, u32[]{:S(2)}) collective-permute-start(f32[32,2176]{1,0:T(8,128)S(1)} %maximum_add_fusion.7), channel_id=1, source_target_pairs={{8,0},{16,8},{24,16},{28,24},{20,28},{12,20},{4,12},{0,4},{9,1},{1... | collective-permute-start | bytes 835592 | tf_op jit(solution)/shard_map/ppermute | solution.py:185
  176.3 11.9 %collective-permute-start.44 = (f32[32,2176]{1,0:T(8,128)S(1)}, f32[32,2176]{1,0:T(8,128)S(1)}, u32[]{:S(2)}, u32[]{:S(2)}) collective-permute-start(f32[32,2176]{1,0:T(8,128)S(1)} %maximum_add_fusion.22), channel_id=1, source_target_pairs={{8,0},{16,8},{24,16},{28,24},{20,28},{12,20},{4,12},{0,4},{9,1},{1... | collective-permute-start | bytes 835592 | tf_op jit(solution)/shard_map/ppermute | solution.py:185
  178.3 11.9 %collective-permute-start.37 = (f32[32,2176]{1,0:T(8,128)S(1)}, f32[32,2176]{1,0:T(8,128)S(1)}, u32[]{:S(2)}, u32[]{:S(2)}) collective-permute-start(f32[32,2176]{1,0:T(8,128)S(1)} %maximum_add_fusion.15), channel_id=1, source_target_pairs={{0,8},{8,16},{16,24},{24,28},{28,20},{20,12},{12,4},{4,0},{1,9},{9... | collective-permute-start | bytes 835592 | tf_op jit(solution)/shard_map/ppermute | solution.py:185
  182.2 11.9 %collective-permute-start.30 = (f32[32,2176]{1,0:T(8,128)S(1)}, f32[32,2176]{1,0:T(8,128)S(1)}, u32[]{:S(2)}, u32[]{:S(2)}) collective-permute-start(f32[32,2176]{1,0:T(8,128)S(1)} %maximum_add_fusion.8), channel_id=1, source_target_pairs={{8,0},{16,8},{24,16},{28,24},{20,28},{12,20},{4,12},{0,4},{9,1},{1... | collective-permute-start | bytes 835592 | tf_op jit(solution)/shard_map/ppermute | solution.py:185
  184.2 11.9 %collective-permute-start.23 = (f32[32,2176]{1,0:T(8,128)S(1)}, f32[32,2176]{1,0:T(8,128)S(1)}, u32[]{:S(2)}, u32[]{:S(2)}) collective-permute-start(f32[32,2176]{1,0:T(8,128)S(1)} %maximum_add_fusion.1), channel_id=1, source_target_pairs={{0,8},{8,16},{16,24},{24,28},{28,20},{20,12},{12,4},{4,0},{1,9},{9... | collective-permute-start | bytes 835592 | tf_op jit(solution)/shard_map/ppermute | solution.py:185
  188.2 11.9 %collective-permute-start.45 = (f32[32,2176]{1,0:T(8,128)S(1)}, f32[32,2176]{1,0:T(8,128)S(1)}, u32[]{:S(2)}, u32[]{:S(2)}) collective-permute-start(f32[32,2176]{1,0:T(8,128)S(1)} %maximum_add_fusion.23), channel_id=1, source_target_pairs={{8,0},{16,8},{24,16},{28,24},{20,28},{12,20},{4,12},{0,4},{9,1},{1... | collective-permute-start | bytes 835592 | tf_op jit(solution)/shard_map/ppermute | solution.py:185
  194.2 11.9 %collective-permute-start.31 = (f32[32,2176]{1,0:T(8,128)S(1)}, f32[32,2176]{1,0:T(8,128)S(1)}, u32[]{:S(2)}, u32[]{:S(2)}) collective-permute-start(f32[32,2176]{1,0:T(8,128)S(1)} %maximum_add_fusion.9), channel_id=1, source_target_pairs={{8,0},{16,8},{24,16},{28,24},{20,28},{12,20},{4,12},{0,4},{9,1},{1... | collective-permute-start | bytes 835592 | tf_op jit(solution)/shard_map/ppermute | solution.py:185
  200.2 11.9 %collective-permute-start.46 = (f32[32,2176]{1,0:T(8,128)S(1)}, f32[32,2176]{1,0:T(8,128)S(1)}, u32[]{:S(2)}, u32[]{:S(2)}) collective-permute-start(f32[32,2176]{1,0:T(8,128)S(1)} %maximum_add_fusion.24), channel_id=1, source_target_pairs={{8,0},{16,8},{24,16},{28,24},{20,28},{12,20},{4,12},{0,4},{9,1},{1... | collective-permute-start | bytes 835592 | tf_op jit(solution)/shard_map/ppermute | solution.py:185
  202.2 11.9 %collective-permute-start.39 = (f32[32,2176]{1,0:T(8,128)S(1)}, f32[32,2176]{1,0:T(8,128)S(1)}, u32[]{:S(2)}, u32[]{:S(2)}) collective-permute-start(f32[32,2176]{1,0:T(8,128)S(1)} %maximum_add_fusion.17), channel_id=1, source_target_pairs={{0,8},{8,16},{16,24},{24,28},{28,20},{20,12},{12,4},{4,0},{1,9},{9... | collective-permute-start | bytes 835592 | tf_op jit(solution)/shard_map/ppermute | solution.py:185
  206.1 11.9 %collective-permute-start.32 = (f32[32,2176]{1,0:T(8,128)S(1)}, f32[32,2176]{1,0:T(8,128)S(1)}, u32[]{:S(2)}, u32[]{:S(2)}) collective-permute-start(f32[32,2176]{1,0:T(8,128)S(1)} %maximum_add_fusion.10), channel_id=1, source_target_pairs={{8,0},{16,8},{24,16},{28,24},{20,28},{12,20},{4,12},{0,4},{9,1},{1... | collective-permute-start | bytes 835592 | tf_op jit(solution)/shard_map/ppermute | solution.py:185
  208.1 11.9 %collective-permute-start.25 = (f32[32,2176]{1,0:T(8,128)S(1)}, f32[32,2176]{1,0:T(8,128)S(1)}, u32[]{:S(2)}, u32[]{:S(2)}) collective-permute-start(f32[32,2176]{1,0:T(8,128)S(1)} %maximum_add_fusion.3), channel_id=1, source_target_pairs={{0,8},{8,16},{16,24},{24,28},{28,20},{20,12},{12,4},{4,0},{1,9},{9... | collective-permute-start | bytes 835592 | tf_op jit(solution)/shard_map/ppermute | solution.py:185
  212.1 11.9 %collective-permute-start.47 = (f32[32,2176]{1,0:T(8,128)S(1)}, f32[32,2176]{1,0:T(8,128)S(1)}, u32[]{:S(2)}, u32[]{:S(2)}) collective-permute-start(f32[32,2176]{1,0:T(8,128)S(1)} %maximum_add_fusion.25), channel_id=1, source_target_pairs={{8,0},{16,8},{24,16},{28,24},{20,28},{12,20},{4,12},{0,4},{9,1},{1... | collective-permute-start | bytes 835592 | tf_op jit(solution)/shard_map/ppermute | solution.py:185
  214.1 11.9 %collective-permute-start.40 = (f32[32,2176]{1,0:T(8,128)S(1)}, f32[32,2176]{1,0:T(8,128)S(1)}, u32[]{:S(2)}, u32[]{:S(2)}) collective-permute-start(f32[32,2176]{1,0:T(8,128)S(1)} %maximum_add_fusion.18), channel_id=1, source_target_pairs={{0,8},{8,16},{16,24},{24,28},{28,20},{20,12},{12,4},{4,0},{1,9},{9... | collective-permute-start | bytes 835592 | tf_op jit(solution)/shard_map/ppermute | solution.py:185
  218.1 11.9 %collective-permute-start.33 = (f32[32,2176]{1,0:T(8,128)S(1)}, f32[32,2176]{1,0:T(8,128)S(1)}, u32[]{:S(2)}, u32[]{:S(2)}) collective-permute-start(f32[32,2176]{1,0:T(8,128)S(1)} %maximum_add_fusion.11), channel_id=1, source_target_pairs={{8,0},{16,8},{24,16},{28,24},{20,28},{12,20},{4,12},{0,4},{9,1},{1... | collective-permute-start | bytes 835592 | tf_op jit(solution)/shard_map/ppermute | solution.py:185
  224.0 11.9 %collective-permute-start.48 = (f32[32,2176]{1,0:T(8,128)S(1)}, f32[32,2176]{1,0:T(8,128)S(1)}, u32[]{:S(2)}, u32[]{:S(2)}) collective-permute-start(f32[32,2176]{1,0:T(8,128)S(1)} %maximum_add_fusion.26), channel_id=1, source_target_pairs={{8,0},{16,8},{24,16},{28,24},{20,28},{12,20},{4,12},{0,4},{9,1},{1... | collective-permute-start | bytes 835592 | tf_op jit(solution)/shard_map/ppermute | solution.py:185
  226.0 11.9 %collective-permute-start.41 = (f32[32,2176]{1,0:T(8,128)S(1)}, f32[32,2176]{1,0:T(8,128)S(1)}, u32[]{:S(2)}, u32[]{:S(2)}) collective-permute-start(f32[32,2176]{1,0:T(8,128)S(1)} %maximum_add_fusion.19), channel_id=1, source_target_pairs={{0,8},{8,16},{16,24},{24,28},{28,20},{20,12},{12,4},{4,0},{1,9},{9... | collective-permute-start | bytes 835592 | tf_op jit(solution)/shard_map/ppermute | solution.py:185
  (50 other events, 273.5 us)
where the time goes:
time: 247 us; the launch traced here: 246 us
  waiting for transfers between devices  109 us (44%)
  starting transfers between devices  57.8 us (23%)
  Pallas kernels  33 us (13%)
  matrix products  28.7 us (12%)
  other arithmetic  11.2 us (5%)
  local copies, waits for them, and re-layouts  4.67 us (2%)
    ppermute x28, waiting for transfers between devices, ring_scatter(): arrived = lax.ppermute(total, 'rows', pairs)  56.1 us
    ppermute x20, waiting for transfers between devices, swap(): return lax.ppermute(value, axis, [(i, i ^ mask) for i in range(size)])  50.4 us
    pallas_call x1, Pallas kernels, inverse_factor(): pl.pallas_call(functools.partial(kernel, scale=scale), out_shape=jax.Shap...  33 us
    ppermute x28, starting transfers between devices, ring_scatter(): arrived = lax.ppermute(total, 'rows', pairs)  30.2 us
    ppermute x20, starting transfers between devices, swap(): return lax.ppermute(value, axis, [(i, i ^ mask) for i in range(size)])  26.8 us
    dot_general x14, matrix products, dot(): lax.dot_general(left_side, right_side, ((contract[:1], contract[1:]), (()...  11.7 us
    dot_general x1, matrix products, on_device(): jnp.dot(late_traits, trait_sketch, preferred_element_type=jnp.float32)  10.7 us
  transfers between devices with their start and end apart: 49, of which 41 were waited for; matrix products, arithmetic and copies ran while one was open for 4% of the time, Pallas kernels for 13%

commit v1 on v0

--- a/solution.py
+++ b/solution.py
@@ -10,6 +10,7 @@
 
 EXACT = lax.Precision.HIGHEST
 CLOSE = lax.Precision.HIGH
+ROUNDS = 3
 
 
 def eliminate(block, out_ref, tall=8):
@@ -26,14 +27,22 @@
         inside = (lanes >= first) & (lanes < first + tall)
         unit = jnp.where(inside, jnp.where(lanes - first == subs - s, 1.0, 0.0), here)
         rows = [jnp.broadcast_to(unit[s + k : s + k + 1, :], shape) for k in range(tall)]
-        inverse, lower = [], {}
-        for i in range(tall):
-            inverse.append(1.0 / a[i][i])
-            for k in range(i + 1, tall):
+        inverse, lower = [None] * tall, {}
+        for i in range(0, tall, 2):
+            p, q, r = a[i][i], a[i + 1][i], a[i + 1][i + 1]
+            both = p * r - q * q
+            inverse[i] = 1.0 / p
+            lower[i + 1, i] = q * inverse[i]
+            inverse[i + 1] = p * (1.0 / both)
+            a[i + 1][i + 1] = r - lower[i + 1, i] * q
+            rows[i + 1] = rows[i + 1] - lower[i + 1, i] * rows[i]
+            for k in range(i + 2, tall):
                 lower[k, i] = a[k][i] * inverse[i]
-                for m in range(i + 1, k + 1):
-                    a[k][m] = a[k][m] - lower[k, i] * a[m][i]
-                rows[k] = rows[k] - lower[k, i] * rows[i]
+                a[k][i + 1] = a[k][i + 1] - lower[k, i] * q
+                lower[k, i + 1] = a[k][i + 1] * inverse[i + 1]
+                for m in range(i + 2, k + 1):
+                    a[k][m] = a[k][m] - lower[k, i] * a[m][i] - lower[k, i + 1] * a[m][i + 1]
+                rows[k] = rows[k] - lower[k, i] * rows[i] - lower[k, i + 1] * rows[i + 1]
         final = rows[0] * lax.rsqrt(a[0][0])
         for i in range(1, tall):
             final = jnp.where(subs == s + i, rows[i] * lax.rsqrt(a[i][i]), final)
@@ -52,7 +61,7 @@
             groups[g] = fresh if g > own else jnp.where(subs >= s + tall, fresh, old)
 
 
-def factor_in_place(ref, small_ref):
+def factor_in_place(ref, small_ref, panel_ref):
     n, width = ref.shape[0], small_ref.shape[0]
     wide = lax.broadcasted_iota(jnp.int32, (width, n), 1)
     deep = lax.broadcasted_iota(jnp.int32, (width, n), 0)
@@ -64,27 +73,34 @@
         inside = (wide >= at) & (wide < at + width)
         panel = jnp.where(inside, jnp.where(wide - at == deep, 1.0, 0.0), panel)
         panel = jnp.dot(small_ref[...], panel, precision=EXACT, preferred_element_type=jnp.float32)
-        below = jnp.where(wide >= at + width, panel, 0.0)
-        update = lax.dot_general(
-            below, panel, (((0,), (0,)), ((), ())), precision=EXACT, preferred_element_type=jnp.float32
-        )
-        for i in range(n // width):
-            old = ref[i * width : (i + 1) * width, :]
-            old = jnp.where(inside & (i > k), 0.0, old)
-            ref[i * width : (i + 1) * width, :] = old - update[i * width : (i + 1) * width, :]
+        panel_ref[...] = panel
         ref[pl.ds(at, width), :] = jnp.where(wide < at + width, panel, 0.0)
+
+        def lower_rows(i, carry):
+            spot = pl.multiple_of(i * width, width)
+            change = lax.dot_general(
+                panel_ref[:, pl.ds(spot, width)],
+                panel,
+                (((0,), (0,)), ((), ())),
+                precision=EXACT,
+                preferred_element_type=jnp.float32,
+            )
+            ref[pl.ds(spot, width), :] = jnp.where(inside, 0.0, ref[pl.ds(spot, width), :]) - change
+            return carry
+
+        lax.fori_loop(k + 1, n // width, lower_rows, 0)
         return carry
 
     lax.fori_loop(0, n // width, step, 0)
 
 
-def factor_whole_kernel(gram_ref, inverse_ref, small_ref, *, scale):
+def factor_whole_kernel(gram_ref, inverse_ref, small_ref, panel_ref, *, scale):
     inverse_ref[...] = gram_ref[...] * scale
-    factor_in_place(inverse_ref, small_ref)
+    factor_in_place(inverse_ref, small_ref, panel_ref)
 
 
 def factor_pieces_kernel(place_ref, *refs, scale):
-    piece_refs, (inverse_ref, small_ref, held_ref) = refs[:4], refs[4:]
+    piece_refs, (inverse_ref, small_ref, panel_ref, held_ref) = refs[:4], refs[4:]
     half = inverse_ref.shape[0] // 2
     rows = half // 2
     for at, piece_ref in enumerate(piece_refs):
@@ -95,13 +111,13 @@
     inverse_ref[:half, half + rows :] = held_ref[1, :, half:]
     inverse_ref[half:, :half] = jnp.zeros((half, half), jnp.float32)
     inverse_ref[half:, half:] = held_ref[1, :, :half]
-    factor_in_place(inverse_ref, small_ref)
+    factor_in_place(inverse_ref, small_ref, panel_ref)
 
 
 def inverse_factor(pieces, place, size, scale):
     width = math.gcd(size, 128)
     vmem = pl.BlockSpec(memory_space=pltpu.VMEM)
-    scratch = [pltpu.VMEM((width, width), jnp.float32)]
+    scratch = [pltpu.VMEM((width, width), jnp.float32), pltpu.VMEM((width, size), jnp.float32)]
     if place is None:
         kernel, specs = factor_whole_kernel, [vmem]
     else:
@@ -187,10 +203,39 @@
     return total
 
 
+def shares(geno_width, trait_width, rounds):
+    tile = math.gcd(math.gcd(geno_width, trait_width), 256) // 2
+    geno_half, trait_half = geno_width // 2, trait_width // 2
+    first = max((geno_half + trait_half) // rounds // tile * tile - geno_half, tile)
+    tiles = (trait_half - first) // tile
+    ends = [first + tiles * at // max(rounds - 1, 1) * tile for at in range(rounds)]
+    ends[-1] = trait_half
+    spans = []
+    for at in range(rounds):
+        for way in range(2):
+            start = ends[at - 1] if at else 0
+            geno = (way * geno_half, (way + 1) * geno_half) if at == 0 else (0, 0)
+            spans.append((geno, (way * trait_half + start, way * trait_half + ends[at])))
+    return spans
+
+
 def sum_rows(value, masks):
     for mask in masks[:-1]:
         value = halve(value, "rows", mask)
-    value = value + swap(value, "rows", masks[-1])
+    moved = swap(value, "rows", masks[-1])
+    value = value + moved
+    for mask in reversed(masks[1:-1]):
+        value = double(value, "rows", mask)
+    return value
+
+
+def whole_sum_rows(value, masks):
+    moved = swap(value, "rows", masks[0])
+    value = value + moved
+    for mask in masks[1:-1]:
+        value = halve(value, "rows", mask)
+    moved = swap(value, "rows", masks[-1])
+    value = value + moved
     for mask in reversed(masks[1:-1]):
         value = double(value, "rows", mask)
     return value
@@ -251,9 +296,9 @@
     sketch_trait = jnp.where(core == 0, other, own)
 
     strip = size // col_count
-    cross_strip = lax.dynamic_slice_in_dim(sketch_geno, (core * chips + chip) * strip, strip, 1)
-    cross = sum_rows(dot(cross_strip, sketch_trait, (0, 0), EXACT), row_masks)
-    cross = double(cross, "rows", row_masks[0])
+    cross_strip = lax.dynamic_slice_in_dim(sketch_geno, col * strip, strip, 1)
+    cross = whole_sum_rows(dot(cross_strip, sketch_trait, (0, 0), EXACT), row_masks)
+    cross = double(cross, "cols", 1)
     for mask in wide_masks:
         cross = double(cross, "cols", mask)
 
@@ -270,7 +315,6 @@
         for mask in wide_masks:
             gram = double(gram, "cols", mask)
         own_inverse = inverse_factor((gram,), None, size, 1.0 / people)
-    cross = double(cross, "cols", 1)
     other_inverse = swap(own_inverse, "cols", 1)
     inverse_geno = jnp.where(core == 0, own_inverse, other_inverse)
     inverse_trait = jnp.where(core == 0, other_inverse, own_inverse)
@@ -291,24 +335,25 @@
 
     pairs = geno_scores.shape[1]
     share = pairs // row_count
-    streams = 4
-    geno_share, trait_share = standardized.shape[1] // streams, traits.shape[1] // streams
+    spans = shares(standardized.shape[1], traits.shape[1], ROUNDS)
     geno_term = term(geno_scores, standardized)
-    summed = []
-    for at in range(streams):
-        trait_term = term(trait_scores, traits[:, at * trait_share : (at + 1) * trait_share])
-        geno_piece = geno_term[:, at * geno_share : (at + 1) * geno_share]
-
-        def take(member, geno_piece=geno_piece, trait_term=trait_term):
-            return jnp.concatenate(
-                [lax.dynamic_slice_in_dim(piece, member * share, share) for piece in (geno_piece, trait_term)],
-                axis=1,
-            )
-
-        summed.append(ring_scatter(take, row_count, at % 2 == 0))
+    geno_sums, trait_sums = [], {}
+    for at, (geno_span, trait_span) in enumerate(spans):
+        trait_term = term(trait_scores, traits[:, slice(*trait_span)])
+        edge = geno_span[1] - geno_span[0]
+        pieces = [geno_term[:, slice(*geno_span)], trait_term] if edge else [trait_term]
+
+        def take(member, pieces=pieces):
+            parts = [lax.dynamic_slice_in_dim(piece, member * share, share) for piece in pieces]
+            return jnp.concatenate(parts, axis=1) if len(parts) > 1 else parts[0]
+
+        total = ring_scatter(take, row_count, at % 2 == 0)
+        if edge:
+            geno_sums.append(total[:, :edge])
+        trait_sums[trait_span] = total[:, edge:]
     root_people = math.sqrt(people)
-    geno_loadings = jnp.concatenate([piece[:, :geno_share] for piece in summed], axis=1) / root_people
-    trait_loadings = jnp.concatenate([piece[:, geno_share:] for piece in summed], axis=1) / root_people
+    geno_loadings = jnp.concatenate(geno_sums, axis=1) / root_people
+    trait_loadings = jnp.concatenate([trait_sums[span] for span in sorted(trait_sums)], axis=1) / root_people
     return (geno_scores, trait_scores, geno_loadings, trait_loadings)
 
 

time: 247 us -> 250 us (1.012)
  starting transfers between devices: 57.8 us -> 68.1 us
  Pallas kernels: 33 us -> 25.7 us
    ppermute x20 -> x19, waiting for transfers between devices: 50.4 us -> 63.6 us  [swap(): return lax.ppermute(value, axis, [(i, i ^ mask) for i in range(size)])]
    ppermute x28 -> x42, starting transfers between devices: 30.2 us -> 42.1 us  [ring_scatter(): arrived = lax.ppermute(total, 'rows', pairs)]
    ppermute x28 -> x42, waiting for transfers between devices: 56.1 us -> 44.3 us  [ring_scatter(): arrived = lax.ppermute(total, 'rows', pairs)]
    pallas_call x1, Pallas kernels: 33 us -> 25.7 us  [inverse_factor(): pl.pallas_call(functools.partial(kernel, scale=scale), out_shape=jax.Shap...]
    ppermute x20 -> x19, starting transfers between devices: 26.8 us -> 25.4 us  [swap(): return lax.ppermute(value, axis, [(i, i ^ mask) for i in range(size)])]
    dot_general x5 -> x7, matrix products: 4.4 us -> 5.16 us  [term(): lax.dot_general(scores, block, (((0,), (0,)), ((), ())), preferred_elemen...]
  transfers between devices with their start and end apart: 49 -> 62, of which waited for: 41 -> 35; matrix products, arithmetic and copies ran while one was open for 4% -> 4% of each run, Pallas kernels for 13% -> 10%
where the time goes in v1:
time: 250 us
  waiting for transfers between devices  110 us (44%)
  starting transfers between devices  68.1 us (27%)
  matrix products  29.3 us (12%)
  Pallas kernels  25.7 us (10%)
  other arithmetic  11.5 us (5%)
  local copies, waits for them, and re-layouts  2.9 us (1%)
    ppermute x19, waiting for transfers between devices, swap(): return lax.ppermute(value, axis, [(i, i ^ mask) for i in range(size)])  63.6 us
    ppermute x42, waiting for transfers between devices, ring_scatter(): arrived = lax.ppermute(total, 'rows', pairs)  44.3 us
    ppermute x42, starting transfers between devices, ring_scatter(): arrived = lax.ppermute(total, 'rows', pairs)  42.1 us
    pallas_call x1, Pallas kernels, inverse_factor(): pl.pallas_call(functools.partial(kernel, scale=scale), out_shape=jax.Shap...  25.7 us
    ppermute x19, starting transfers between devices, swap(): return lax.ppermute(value, axis, [(i, i ^ mask) for i in range(size)])  25.4 us
    dot_general x14, matrix products, dot(): lax.dot_general(left_side, right_side, ((contract[:1], contract[1:]), (()...  11.6 us
    dot_general x1, matrix products, on_device(): jnp.dot(late_traits, trait_sketch, preferred_element_type=jnp.float32)  10.7 us
    dot_general x7, matrix products, term(): lax.dot_general(scores, block, (((0,), (0,)), ((), ())), preferred_elemen...  5.16 us
  transfers between devices with their start and end apart: 62, of which 35 were waited for; matrix products, arithmetic and copies ran while one was open for 4% of the time, Pallas kernels for 10%

profile of v1, /device:TPU:0, one launch (start us, length us, event | category | flops | bytes accessed | tf_op | source)
XLA Modules:
  0.0 249.9 jit_solution(158263021392970743)
XLA Ops:
  6.0 10.7 %fusion.39 = f32[640,512]{1,0:T(8,128)S(1)} fusion(bf16[640,8192]{1,0:T(8,128)(2,1)} %param.8, bf16[8192,512]{1,0:T(8,128)(2,1)} %param.10), kind=kOutput, calls=%fused_computation.166 | convolution fusion | flops 5368709120 | bytes 20185088 | tf_op jit(solution)/shard_map/dot_general | solution.py:266
  17.2 2.6 %collective-permute-start.1 = (f32[320,512]{1,0:T(8,128)S(1)}, f32[320,512]{1,0:T(8,128)S(1)}, u32[]{:S(2)}, u32[]{:S(2)}) collective-permute-start(f32[320,512]{1,0:T(8,128)S(1)} %dynamic-slice_add_fusion.1), channel_id=1, source_target_pairs={{0,2},{1,3},{2,0},{3,1},{4,6},{5,7},{6,4},{7,5},{8,10},{9,11},{10,... | collective-permute-start | bytes 1966088 | tf_op jit(solution)/shard_map/ppermute | solution.py:162
  21.9 13.4 %collective-permute-done.1 = f32[320,512]{1,0:T(8,128)S(1)} collective-permute-done((f32[320,512]{1,0:T(8,128)S(1)}, f32[320,512]{1,0:T(8,128)S(1)}, u32[]{:S(2)}, u32[]{:S(2)}) %collective-permute-start.1) | collective-permute-done | bytes 655392 | tf_op jit(solution)/shard_map/ppermute | solution.py:162
  35.4 13.8 %collective-permute-done.3 = f32[320,512]{1,0:T(8,128)} collective-permute-done((f32[320,512]{1,0:T(8,128)S(1)}, f32[320,512]{1,0:T(8,128)}, u32[]{:S(2)}, u32[]{:S(2)}) %collective-permute-start.3) | collective-permute-done | bytes 655392 | tf_op jit(solution)/shard_map/ppermute | solution.py:162
  59.8 3.6 %collective-permute-done.6 = f32[128,384]{1,0:T(8,128)} collective-permute-done((f32[128,384]{1,0:T(8,128)S(1)}, f32[128,384]{1,0:T(8,128)}, u32[]{:S(2)}, u32[]{:S(2)}) %collective-permute-start.6) | collective-permute-done | bytes 196640 | tf_op jit(solution)/shard_map/ppermute | solution.py:162
  66.3 2.8 %collective-permute-done.7 = f32[64,384]{1,0:T(8,128)S(1)} collective-permute-done((f32[64,384]{1,0:T(8,128)S(1)}, f32[64,384]{1,0:T(8,128)S(1)}, u32[]{:S(2)}, u32[]{:S(2)}) %collective-permute-start.7) | collective-permute-done | bytes 98336 | tf_op jit(solution)/shard_map/ppermute | solution.py:162
  69.1 2.9 %collective-permute-start.8 = (f32[64,384]{1,0:T(8,128)S(1)}, f32[64,384]{1,0:T(8,128)S(1)}, u32[]{:S(2)}, u32[]{:S(2)}) collective-permute-start(f32[64,384]{1,0:T(8,128)S(1)} %dynamic-slice_add_fusion.28), channel_id=1, source_target_pairs={{0,16},{4,20},{8,24},{12,28},{16,0},{20,4},{24,8},{28,12},{1,17},{... | collective-permute-start | bytes 294920 | tf_op jit(solution)/shard_map/ppermute | solution.py:162
  76.7 3.0 %collective-permute-done.9 = f32[64,384]{1,0:T(8,128)S(1)} collective-permute-done((f32[64,384]{1,0:T(8,128)S(1)}, f32[64,384]{1,0:T(8,128)S(1)}, u32[]{:S(2)}, u32[]{:S(2)}) %collective-permute-start.9) | collective-permute-done | bytes 98336 | tf_op jit(solution)/shard_map/ppermute | solution.py:162
  86.9 2.5 %collective-permute-done.12.refs_3_ = f32[128,384]{1,0:T(8,128)} collective-permute-done((f32[128,384]{1,0:T(8,128)S(1)}, f32[128,384]{1,0:T(8,128)}, u32[]{:S(2)}, u32[]{:S(2)}) %collective-permute-start.12) | collective-permute-done | bytes 196640 | tf_op jit(solution)/shard_map/ppermute | solution.py:310
  89.4 25.7 %inverse_factor.1 = f32[512,512]{1,0:T(8,128)} custom-call(s32[2]{0:T(128)} %pad_add_fusion.place_ref, f32[128,384]{1,0:T(8,128)} %copy-done.13, f32[128,384]{1,0:T(8,128)} %copy-done.15, f32[128,384]{1,0:T(8,128)} %copy-done.16, f32[128,384]{1,0:T(8,128)} %collective-permute-done.12.refs_3_), custom_call_target="tpu_custom_call" | custom-call | tf_op jit(solution)/shard_map/inverse_factor/pallas_call | solution.py:127
  116.0 3.2 %collective-permute-start.16 = (f32[64,512]{1,0:T(8,128)S(1)}, f32[64,512]{1,0:T(8,128)S(1)}, u32[]{:S(2)}, u32[]{:S(2)}) collective-permute-start(f32[64,512]{1,0:T(8,128)S(1)} %dynamic-slice_add_fusion.27), channel_id=1, source_target_pairs={{0,16},{4,20},{8,24},{12,28},{16,0},{20,4},{24,8},{28,12},{1,17},{... | collective-permute-start | bytes 393224 | tf_op jit(solution)/shard_map/ppermute | solution.py:162
  119.2 7.0 %collective-permute-done.16 = f32[64,512]{1,0:T(8,128)S(1)} collective-permute-done((f32[64,512]{1,0:T(8,128)S(1)}, f32[64,512]{1,0:T(8,128)S(1)}, u32[]{:S(2)}, u32[]{:S(2)}) %collective-permute-start.16) | collective-permute-done | bytes 131104 | tf_op jit(solution)/shard_map/ppermute | solution.py:162
  127.0 4.5 %collective-permute-done.17 = f32[64,512]{1,0:T(8,128)S(1)} collective-permute-done((f32[64,512]{1,0:T(8,128)S(1)}, f32[64,512]{1,0:T(8,128)S(1)}, u32[]{:S(2)}, u32[]{:S(2)}) %collective-permute-start.17) | collective-permute-done | bytes 131104 | tf_op jit(solution)/shard_map/ppermute | solution.py:162
  137.1 10.1 %collective-permute-done.19 = f32[256,512]{1,0:T(8,128)S(1)} collective-permute-done((f32[256,512]{1,0:T(8,128)S(1)}, f32[256,512]{1,0:T(8,128)S(1)}, u32[]{:S(2)}, u32[]{:S(2)}) %collective-permute-start.19) | collective-permute-done | bytes 524320 | tf_op jit(solution)/shard_map/ppermute | solution.py:162
  169.8 3.1 %collective-permute-done.34 = f32[32,1408]{1,0:T(8,128)S(1)} collective-permute-done((f32[32,1408]{1,0:T(8,128)S(1)}, f32[32,1408]{1,0:T(8,128)S(1)}, u32[]{:S(2)}, u32[]{:S(2)}) %collective-permute-start.34) | collective-permute-done | bytes 180256 | tf_op jit(solution)/shard_map/ppermute | solution.py:201
  175.0 2.1 collective-permute-done.41
  182.5 2.3 collective-permute-done.35
  186.9 2.1 collective-permute-done.42
  198.9 2.1 collective-permute-done.43
  210.8 2.1 collective-permute-done.44
  222.7 2.1 collective-permute-done.45
  234.7 2.1 collective-permute-done.46
  241.4 3.0 %collective-permute-done.40 = f32[32,1408]{1,0:T(8,128)S(1)} collective-permute-done((f32[32,1408]{1,0:T(8,128)S(1)}, f32[32,1408]{1,0:T(8,128)S(1)}, u32[]{:S(2)}, u32[]{:S(2)}) %collective-permute-start.40) | collective-permute-done | bytes 180256 | tf_op jit(solution)/shard_map/ppermute | solution.py:201
  245.2 3.5 %collective-permute-done.47 = f32[32,1536]{1,0:T(8,128)S(1)} collective-permute-done((f32[32,1536]{1,0:T(8,128)S(1)}, f32[32,1536]{1,0:T(8,128)S(1)}, u32[]{:S(2)}, u32[]{:S(2)}) %collective-permute-start.47) | collective-permute-done | bytes 196640 | tf_op jit(solution)/shard_map/ppermute | solution.py:201
  (256 shorter events, 117.8 us)
Async XLA Ops:
  17.2 18.2 %collective-permute-start.1 = (f32[320,512]{1,0:T(8,128)S(1)}, f32[320,512]{1,0:T(8,128)S(1)}, u32[]{:S(2)}, u32[]{:S(2)}) collective-permute-start(f32[320,512]{1,0:T(8,128)S(1)} %dynamic-slice_add_fusion.1), channel_id=1, source_target_pairs={{0,2},{1,3},{2,0},{3,1},{4,6},{5,7},{6,4},{7,5},{8,10},{9,11},{10,... | collective-permute-start | bytes 1966088 | tf_op jit(solution)/shard_map/ppermute | solution.py:162
  19.9 29.3 %collective-permute-start.3 = (f32[320,512]{1,0:T(8,128)S(1)}, f32[320,512]{1,0:T(8,128)}, u32[]{:S(2)}, u32[]{:S(2)}) collective-permute-start(f32[320,512]{1,0:T(8,128)S(1)} %dynamic-slice_add_fusion), channel_id=1, source_target_pairs={{0,2},{1,3},{2,0},{3,1},{4,6},{5,7},{6,4},{7,5},{8,10},{9,11},{10,... | collective-permute-start | bytes 1966088 | tf_op jit(solution)/shard_map/ppermute | solution.py:162
  58.1 13.9 %collective-permute-start.5 = (f32[320,512]{1,0:T(8,128)S(1)}, f32[320,512]{1,0:T(8,128)S(1)}, u32[]{:S(2)}, u32[]{:S(2)}) collective-permute-start(f32[320,512]{1,0:T(8,128)S(1)} %get-tuple-element.12), channel_id=1, source_target_pairs={{0,1},{1,0},{2,3},{3,2},{4,5},{5,4},{6,7},{7,6},{8,9},{9,8},{10,11... | collective-permute-start | bytes 1966088 | tf_op jit(solution)/shard_map/ppermute | solution.py:162
  84.0 31.1 %collective-permute-start.15 = (f32[64,512]{1,0:T(8,128)}, f32[64,512]{1,0:T(8,128)}, u32[]{:S(2)}, u32[]{:S(2)}) collective-permute-start(f32[64,512]{1,0:T(8,128)} %constant_dynamic-slice_fusion.36), channel_id=1, source_target_pairs={{0,8},{4,12},{8,0},{12,4},{16,24},{20,28},{24,16},{28,20},{1,9},{5... | collective-permute-start | bytes 393224 | tf_op jit(solution)/shard_map/ppermute | solution.py:162
  115.1 19.5 %collective-permute-start.13 = (f32[512,512]{1,0:T(8,128)}, f32[512,512]{1,0:T(8,128)}, u32[]{:S(2)}, u32[]{:S(2)}) collective-permute-start(f32[512,512]{1,0:T(8,128)} %inverse_factor.1), channel_id=1, source_target_pairs={{0,1},{1,0},{2,3},{3,2},{4,5},{5,4},{6,7},{7,6},{8,9},{9,8},{10,11... | collective-permute-start | bytes 3145736 | tf_op jit(solution)/shard_map/ppermute | solution.py:162
  133.2 14.0 %collective-permute-start.19 = (f32[256,512]{1,0:T(8,128)S(1)}, f32[256,512]{1,0:T(8,128)S(1)}, u32[]{:S(2)}, u32[]{:S(2)}) collective-permute-start(f32[256,512]{1,0:T(8,128)S(1)} %constant_dynamic-update-slice_fusion.1), channel_id=1, source_target_pairs={{0,2},{1,3},{2,0},{3,1},{4,6},{5,7},{6,4},{7,5},{8,10},{9,11},{10,... | collective-permute-start | bytes 1572872 | tf_op jit(solution)/shard_map/ppermute | solution.py:162
  163.7 13.4 %collective-permute-start.41 = (f32[32,1536]{1,0:T(8,128)S(1)}, f32[32,1536]{1,0:T(8,128)S(1)}, u32[]{:S(2)}, u32[]{:S(2)}) collective-permute-start(f32[32,1536]{1,0:T(8,128)S(1)} %constant_dynamic-slice_fusion.2), channel_id=1, source_target_pairs={{0,8},{8,16},{16,24},{24,28},{28,20},{20,12},{12,4},{4,0},{1,9},{9... | collective-permute-start | bytes 589832 | tf_op jit(solution)/shard_map/ppermute | solution.py:201
  169.0 12.2 %collective-permute-start.28 = (f32[32,1408]{1,0:T(8,128)S(1)}, f32[32,1408]{1,0:T(8,128)S(1)}, u32[]{:S(2)}, u32[]{:S(2)}) collective-permute-start(f32[32,1408]{1,0:T(8,128)S(1)} %maximum_add_fusion.7), channel_id=1, source_target_pairs={{8,0},{16,8},{24,16},{28,24},{20,28},{12,20},{4,12},{0,4},{9,1},{1... | collective-permute-start | bytes 540680 | tf_op jit(solution)/shard_map/ppermute | solution.py:201
  173.7 11.1 %collective-permute-start.35 = (f32[32,1408]{1,0:T(8,128)S(1)}, f32[32,1408]{1,0:T(8,128)S(1)}, u32[]{:S(2)}, u32[]{:S(2)}) collective-permute-start(f32[32,1408]{1,0:T(8,128)S(1)} %dynamic-slice_add_fusion.26), channel_id=1, source_target_pairs={{0,8},{8,16},{16,24},{24,28},{28,20},{20,12},{12,4},{4,0},{1,9},{9... | collective-permute-start | bytes 540680 | tf_op jit(solution)/shard_map/ppermute | solution.py:201
  177.9 11.1 %collective-permute-start.42 = (f32[32,1536]{1,0:T(8,128)S(1)}, f32[32,1536]{1,0:T(8,128)S(1)}, u32[]{:S(2)}, u32[]{:S(2)}) collective-permute-start(f32[32,1536]{1,0:T(8,128)S(1)} %dynamic-slice_add_fusion.13), channel_id=1, source_target_pairs={{0,8},{8,16},{16,24},{24,28},{28,20},{20,12},{12,4},{4,0},{1,9},{9... | collective-permute-start | bytes 589832 | tf_op jit(solution)/shard_map/ppermute | solution.py:201
  181.3 11.9 %collective-permute-start.29 = (f32[32,1408]{1,0:T(8,128)S(1)}, f32[32,1408]{1,0:T(8,128)S(1)}, u32[]{:S(2)}, u32[]{:S(2)}) collective-permute-start(f32[32,1408]{1,0:T(8,128)S(1)} %maximum_add_fusion.8), channel_id=1, source_target_pairs={{8,0},{16,8},{24,16},{28,24},{20,28},{12,20},{4,12},{0,4},{9,1},{1... | collective-permute-start | bytes 540680 | tf_op jit(solution)/shard_map/ppermute | solution.py:201
  189.8 11.1 %collective-permute-start.43 = (f32[32,1536]{1,0:T(8,128)S(1)}, f32[32,1536]{1,0:T(8,128)S(1)}, u32[]{:S(2)}, u32[]{:S(2)}) collective-permute-start(f32[32,1536]{1,0:T(8,128)S(1)} %dynamic-slice_add_fusion.12), channel_id=1, source_target_pairs={{0,8},{8,16},{16,24},{24,28},{28,20},{20,12},{12,4},{4,0},{1,9},{9... | collective-permute-start | bytes 589832 | tf_op jit(solution)/shard_map/ppermute | solution.py:201
  193.3 11.8 %collective-permute-start.30 = (f32[32,1408]{1,0:T(8,128)S(1)}, f32[32,1408]{1,0:T(8,128)S(1)}, u32[]{:S(2)}, u32[]{:S(2)}) collective-permute-start(f32[32,1408]{1,0:T(8,128)S(1)} %maximum_add_fusion.9), channel_id=1, source_target_pairs={{8,0},{16,8},{24,16},{28,24},{20,28},{12,20},{4,12},{0,4},{9,1},{1... | collective-permute-start | bytes 540680 | tf_op jit(solution)/shard_map/ppermute | solution.py:201
  201.7 11.1 %collective-permute-start.44 = (f32[32,1536]{1,0:T(8,128)S(1)}, f32[32,1536]{1,0:T(8,128)S(1)}, u32[]{:S(2)}, u32[]{:S(2)}) collective-permute-start(f32[32,1536]{1,0:T(8,128)S(1)} %dynamic-slice_add_fusion.11), channel_id=1, source_target_pairs={{0,8},{8,16},{16,24},{24,28},{28,20},{20,12},{12,4},{4,0},{1,9},{9... | collective-permute-start | bytes 589832 | tf_op jit(solution)/shard_map/ppermute | solution.py:201
  205.3 11.8 %collective-permute-start.31 = (f32[32,1408]{1,0:T(8,128)S(1)}, f32[32,1408]{1,0:T(8,128)S(1)}, u32[]{:S(2)}, u32[]{:S(2)}) collective-permute-start(f32[32,1408]{1,0:T(8,128)S(1)} %maximum_add_fusion.10), channel_id=1, source_target_pairs={{8,0},{16,8},{24,16},{28,24},{20,28},{12,20},{4,12},{0,4},{9,1},{1... | collective-permute-start | bytes 540680 | tf_op jit(solution)/shard_map/ppermute | solution.py:201
  209.5 11.1 %collective-permute-start.38 = (f32[32,1408]{1,0:T(8,128)S(1)}, f32[32,1408]{1,0:T(8,128)S(1)}, u32[]{:S(2)}, u32[]{:S(2)}) collective-permute-start(f32[32,1408]{1,0:T(8,128)S(1)} %dynamic-slice_add_fusion.23), channel_id=1, source_target_pairs={{0,8},{8,16},{16,24},{24,28},{28,20},{20,12},{12,4},{4,0},{1,9},{9... | collective-permute-start | bytes 540680 | tf_op jit(solution)/shard_map/ppermute | solution.py:201
  213.7 11.1 %collective-permute-start.45 = (f32[32,1536]{1,0:T(8,128)S(1)}, f32[32,1536]{1,0:T(8,128)S(1)}, u32[]{:S(2)}, u32[]{:S(2)}) collective-permute-start(f32[32,1536]{1,0:T(8,128)S(1)} %dynamic-slice_add_fusion.10), channel_id=1, source_target_pairs={{0,8},{8,16},{16,24},{24,28},{28,20},{20,12},{12,4},{4,0},{1,9},{9... | collective-permute-start | bytes 589832 | tf_op jit(solution)/shard_map/ppermute | solution.py:201
  217.2 11.8 %collective-permute-start.32 = (f32[32,1408]{1,0:T(8,128)S(1)}, f32[32,1408]{1,0:T(8,128)S(1)}, u32[]{:S(2)}, u32[]{:S(2)}) collective-permute-start(f32[32,1408]{1,0:T(8,128)S(1)} %maximum_add_fusion.11), channel_id=1, source_target_pairs={{8,0},{16,8},{24,16},{28,24},{20,28},{12,20},{4,12},{0,4},{9,1},{1... | collective-permute-start | bytes 540680 | tf_op jit(solution)/shard_map/ppermute | solution.py:201
  221.5 11.1 %collective-permute-start.39 = (f32[32,1408]{1,0:T(8,128)S(1)}, f32[32,1408]{1,0:T(8,128)S(1)}, u32[]{:S(2)}, u32[]{:S(2)}) collective-permute-start(f32[32,1408]{1,0:T(8,128)S(1)} %dynamic-slice_add_fusion.22), channel_id=1, source_target_pairs={{0,8},{8,16},{16,24},{24,28},{28,20},{20,12},{12,4},{4,0},{1,9},{9... | collective-permute-start | bytes 540680 | tf_op jit(solution)/shard_map/ppermute | solution.py:201
  225.6 11.1 %collective-permute-start.46 = (f32[32,1536]{1,0:T(8,128)S(1)}, f32[32,1536]{1,0:T(8,128)S(1)}, u32[]{:S(2)}, u32[]{:S(2)}) collective-permute-start(f32[32,1536]{1,0:T(8,128)S(1)} %dynamic-slice_add_fusion.9), channel_id=1, source_target_pairs={{0,8},{8,16},{16,24},{24,28},{28,20},{20,12},{12,4},{4,0},{1,9},{9... | collective-permute-start | bytes 589832 | tf_op jit(solution)/shard_map/ppermute | solution.py:201
  229.2 15.3 %collective-permute-start.33 = (f32[32,1408]{1,0:T(8,128)S(1)}, f32[32,1408]{1,0:T(8,128)S(1)}, u32[]{:S(2)}, u32[]{:S(2)}) collective-permute-start(f32[32,1408]{1,0:T(8,128)S(1)} %maximum_add_fusion.12), channel_id=1, source_target_pairs={{8,0},{16,8},{24,16},{28,24},{20,28},{12,20},{4,12},{0,4},{9,1},{1... | collective-permute-start | bytes 540680 | tf_op jit(solution)/shard_map/ppermute | solution.py:201
  233.4 11.1 %collective-permute-start.40 = (f32[32,1408]{1,0:T(8,128)S(1)}, f32[32,1408]{1,0:T(8,128)S(1)}, u32[]{:S(2)}, u32[]{:S(2)}) collective-permute-start(f32[32,1408]{1,0:T(8,128)S(1)} %dynamic-slice_add_fusion.21), channel_id=1, source_target_pairs={{0,8},{8,16},{16,24},{24,28},{28,20},{20,12},{12,4},{4,0},{1,9},{9... | collective-permute-start | bytes 540680 | tf_op jit(solution)/shard_map/ppermute | solution.py:201
  236.7 12.0 %collective-permute-start.54 = (f32[32,1408]{1,0:T(8,128)S(1)}, f32[32,1408]{1,0:T(8,128)S(1)}, u32[]{:S(2)}, u32[]{:S(2)}) collective-permute-start(f32[32,1408]{1,0:T(8,128)S(1)} %dynamic-slice_add_fusion.15), channel_id=1, source_target_pairs={{8,0},{16,8},{24,16},{28,24},{20,28},{12,20},{4,12},{0,4},{9,1},{1... | collective-permute-start | bytes 540680 | tf_op jit(solution)/shard_map/ppermute | solution.py:201
  237.6 11.1 %collective-permute-start.47 = (f32[32,1536]{1,0:T(8,128)S(1)}, f32[32,1536]{1,0:T(8,128)S(1)}, u32[]{:S(2)}, u32[]{:S(2)}) collective-permute-start(f32[32,1536]{1,0:T(8,128)S(1)} %dynamic-slice_add_fusion.8), channel_id=1, source_target_pairs={{0,8},{8,16},{16,24},{24,28},{28,20},{20,12},{12,4},{4,0},{1,9},{9... | collective-permute-start | bytes 589832 | tf_op jit(solution)/shard_map/ppermute | solution.py:201
  (58 other events, 375.5 us)

commit v2 on v1

--- a/solution.py
+++ b/solution.py
@@ -263,16 +263,22 @@
     chip_geno = halve(partial_geno, "cols", 1)
     height = genotypes.shape[0] // 2
     late_traits, chip_geno = lax.optimization_barrier((traits, chip_geno))
-    partial_trait = jnp.dot(late_traits, trait_sketch, preferred_element_type=jnp.float32)
     half_geno = over_chips(chip_geno)
-    half_trait = over_chips(halve(partial_trait, "cols", 1))
+    parts = []
+    for at in range(2):
+        span = slice(at * (size // 2), (at + 1) * (size // 2))
+        part = jnp.dot(late_traits, trait_sketch[:, span], preferred_element_type=jnp.float32)
+        chip_part = halve(part, "cols", 1)
+        late_traits, chip_part = lax.optimization_barrier((late_traits, chip_part))
+        parts.append(over_chips(chip_part))
+    half_trait = jnp.concatenate(parts, axis=1)
 
     mine = jnp.where(core == 0, half_geno, half_trait)
     others = jnp.where(core == 0, half_trait, half_geno)
     arrived = swap(others, "cols", 1)
 
     def gram_of(left_of, right_of):
-        return sum(dot(left_of(view), right_of(view), (0, 0), EXACT) for view in (mine, arrived))
+        return sum(dot(left_of(view), right_of(view), (0, 0), CLOSE) for view in (mine, arrived))
 
     def columns(at, width):
         return lambda view: lax.dynamic_slice_in_dim(view, at, width, 1)
@@ -297,7 +303,7 @@
 
     strip = size // col_count
     cross_strip = lax.dynamic_slice_in_dim(sketch_geno, col * strip, strip, 1)
-    cross = whole_sum_rows(dot(cross_strip, sketch_trait, (0, 0), EXACT), row_masks)
+    cross = whole_sum_rows(dot(cross_strip, sketch_trait, (0, 0), CLOSE), row_masks)
     cross = double(cross, "cols", 1)
     for mask in wide_masks:
         cross = double(cross, "cols", mask)

time: 250 us -> 251 us (level)
    dot_general x1 -> x2, matrix products: 10.7 us -> 12 us  [on_device(): jnp.dot(late_traits, trait_sketch[:, span], preferred_element_type=jnp.fl...]
    ppermute x19 -> x21, waiting for transfers between devices: 63.6 us -> 64.6 us  [swap(): return lax.ppermute(value, axis, [(i, i ^ mask) for i in range(size)])]
    ppermute x19 -> x21, starting transfers between devices: 25.4 us -> 26.1 us  [swap(): return lax.ppermute(value, axis, [(i, i ^ mask) for i in range(size)])]
  transfers between devices with their start and end apart: 62 -> 64, of which waited for: 35 -> 36; matrix products, arithmetic and copies ran while one was open for 4% -> 4% of each run, Pallas kernels for 10% -> 10%
where the time goes in v2:
time: 251 us
  waiting for transfers between devices  111 us (44%)
  starting transfers between devices  68.7 us (27%)
  matrix products  28.9 us (12%)
  Pallas kernels  25.7 us (10%)
  other arithmetic  10.3 us (4%)
  local copies, waits for them, and re-layouts  3.37 us (1%)
    ppermute x21, waiting for transfers between devices, swap(): return lax.ppermute(value, axis, [(i, i ^ mask) for i in range(size)])  64.6 us
    ppermute x42, waiting for transfers between devices, ring_scatter(): arrived = lax.ppermute(total, 'rows', pairs)  44.3 us
    ppermute x42, starting transfers between devices, ring_scatter(): arrived = lax.ppermute(total, 'rows', pairs)  42.1 us
    ppermute x21, starting transfers between devices, swap(): return lax.ppermute(value, axis, [(i, i ^ mask) for i in range(size)])  26.1 us
    pallas_call x1, Pallas kernels, inverse_factor(): pl.pallas_call(functools.partial(kernel, scale=scale), out_shape=jax.Shap...  25.7 us
    dot_general x2, matrix products, on_device(): jnp.dot(late_traits, trait_sketch[:, span], preferred_element_type=jnp.fl...  12 us
    dot_general x14, matrix products, dot(): lax.dot_general(left_side, right_side, ((contract[:1], contract[1:]), (()...  9.87 us
    dot_general x7, matrix products, term(): lax.dot_general(scores, block, (((0,), (0,)), ((), ())), preferred_elemen...  5.16 us
  transfers between devices with their start and end apart: 64, of which 36 were waited for; matrix products, arithmetic and copies ran while one was open for 4% of the time, Pallas kernels for 10%

profile of v2, /device:TPU:0, one launch (start us, length us, event | category | flops | bytes accessed | tf_op | source)
XLA Modules:
  0.0 250.5 jit_solution(8015996577865803976)
XLA Ops:
  6.0 7.0 %fusion.2 = f32[640,256]{1,0:T(8,128)S(1)} fusion(bf16[640,8192]{1,0:T(8,128)(2,1)} %param.8, bf16[8192,512]{1,0:T(8,128)(2,1)} %param.10), kind=kOutput, calls=%fused_computation.2 | convolution fusion | flops 2684354560 | bytes 15335424 | tf_op jit(solution)/shard_map/dot_general | solution.py:270
  14.8 5.1 %fusion = f32[640,256]{1,0:T(8,128)S(1)} fusion(bf16[640,8192]{1,0:T(8,128)(2,1)S(1)} %bitcast.26, bf16[8192,512]{1,0:T(8,128)(2,1)} %param.10), kind=kOutput, calls=%fused_computation | convolution fusion | flops 2684354560 | bytes 15335424 | tf_op jit(solution)/shard_map/dot_general | solution.py:270
  20.4 2.6 %collective-permute-start.1 = (f32[320,512]{1,0:T(8,128)S(1)}, f32[320,512]{1,0:T(8,128)S(1)}, u32[]{:S(2)}, u32[]{:S(2)}) collective-permute-start(f32[320,512]{1,0:T(8,128)S(1)} %dynamic-slice_add_fusion), channel_id=1, source_target_pairs={{0,2},{1,3},{2,0},{3,1},{4,6},{5,7},{6,4},{7,5},{8,10},{9,11},{10,... | collective-permute-start | bytes 1966088 | tf_op jit(solution)/shard_map/ppermute | solution.py:162
  23.1 2.1 collective-permute-start.5
  25.1 20.5 %collective-permute-done.3 = f32[320,256]{1,0:T(8,128)S(1)} collective-permute-done((f32[320,256]{1,0:T(8,128)S(1)}, f32[320,256]{1,0:T(8,128)S(1)}, u32[]{:S(2)}, u32[]{:S(2)}) %collective-permute-start.3) | collective-permute-done | bytes 327712 | tf_op jit(solution)/shard_map/ppermute | solution.py:162
  45.6 6.7 %collective-permute-done.5 = f32[320,256]{1,0:T(8,128)S(1)} collective-permute-done((f32[320,256]{1,0:T(8,128)S(1)}, f32[320,256]{1,0:T(8,128)S(1)}, u32[]{:S(2)}, u32[]{:S(2)}) %collective-permute-start.5) | collective-permute-done | bytes 327712 | tf_op jit(solution)/shard_map/ppermute | solution.py:162
  60.5 3.5 %collective-permute-done.8 = f32[128,384]{1,0:T(8,128)} collective-permute-done((f32[128,384]{1,0:T(8,128)S(1)}, f32[128,384]{1,0:T(8,128)}, u32[]{:S(2)}, u32[]{:S(2)}) %collective-permute-start.8) | collective-permute-done | bytes 196640 | tf_op jit(solution)/shard_map/ppermute | solution.py:162
  66.9 2.8 %collective-permute-done.9 = f32[64,384]{1,0:T(8,128)S(1)} collective-permute-done((f32[64,384]{1,0:T(8,128)S(1)}, f32[64,384]{1,0:T(8,128)S(1)}, u32[]{:S(2)}, u32[]{:S(2)}) %collective-permute-start.9) | collective-permute-done | bytes 98336 | tf_op jit(solution)/shard_map/ppermute | solution.py:162
  69.7 2.9 %collective-permute-start.10 = (f32[64,384]{1,0:T(8,128)S(1)}, f32[64,384]{1,0:T(8,128)S(1)}, u32[]{:S(2)}, u32[]{:S(2)}) collective-permute-start(f32[64,384]{1,0:T(8,128)S(1)} %dynamic-slice_add_fusion.29), channel_id=1, source_target_pairs={{0,16},{4,20},{8,24},{12,28},{16,0},{20,4},{24,8},{28,12},{1,17},{... | collective-permute-start | bytes 294920 | tf_op jit(solution)/shard_map/ppermute | solution.py:162
  77.3 2.9 %collective-permute-done.11 = f32[64,384]{1,0:T(8,128)S(1)} collective-permute-done((f32[64,384]{1,0:T(8,128)S(1)}, f32[64,384]{1,0:T(8,128)S(1)}, u32[]{:S(2)}, u32[]{:S(2)}) %collective-permute-start.11) | collective-permute-done | bytes 98336 | tf_op jit(solution)/shard_map/ppermute | solution.py:162
  87.5 2.5 collective-permute-done.14.refs_3_
  90.0 25.7 %inverse_factor.1 = f32[512,512]{1,0:T(8,128)} custom-call(s32[2]{0:T(128)} %pad_add_fusion.place_ref, f32[128,384]{1,0:T(8,128)} %copy-done.13, f32[128,384]{1,0:T(8,128)} %copy-done.15, f32[128,384]{1,0:T(8,128)} %copy-done.16, f32[128,384]{1,0:T(8,128)} %collective-permute-done.14.refs_3_), custom_call_target="tpu_custom_call" | custom-call | tf_op jit(solution)/shard_map/inverse_factor/pallas_call | solution.py:127
  116.6 3.2 %collective-permute-start.18 = (f32[64,512]{1,0:T(8,128)S(1)}, f32[64,512]{1,0:T(8,128)S(1)}, u32[]{:S(2)}, u32[]{:S(2)}) collective-permute-start(f32[64,512]{1,0:T(8,128)S(1)} %dynamic-slice_add_fusion.28), channel_id=1, source_target_pairs={{0,16},{4,20},{8,24},{12,28},{16,0},{20,4},{24,8},{28,12},{1,17},{... | collective-permute-start | bytes 393224 | tf_op jit(solution)/shard_map/ppermute | solution.py:162
  119.8 7.0 %collective-permute-done.18 = f32[64,512]{1,0:T(8,128)S(1)} collective-permute-done((f32[64,512]{1,0:T(8,128)S(1)}, f32[64,512]{1,0:T(8,128)S(1)}, u32[]{:S(2)}, u32[]{:S(2)}) %collective-permute-start.18) | collective-permute-done | bytes 131104 | tf_op jit(solution)/shard_map/ppermute | solution.py:162
  127.6 4.5 %collective-permute-done.19 = f32[64,512]{1,0:T(8,128)S(1)} collective-permute-done((f32[64,512]{1,0:T(8,128)S(1)}, f32[64,512]{1,0:T(8,128)S(1)}, u32[]{:S(2)}, u32[]{:S(2)}) %collective-permute-start.19) | collective-permute-done | bytes 131104 | tf_op jit(solution)/shard_map/ppermute | solution.py:162
  137.7 10.1 %collective-permute-done.21 = f32[256,512]{1,0:T(8,128)S(1)} collective-permute-done((f32[256,512]{1,0:T(8,128)S(1)}, f32[256,512]{1,0:T(8,128)S(1)}, u32[]{:S(2)}, u32[]{:S(2)}) %collective-permute-start.21) | collective-permute-done | bytes 524320 | tf_op jit(solution)/shard_map/ppermute | solution.py:162
  170.4 3.1 %collective-permute-done.36 = f32[32,1408]{1,0:T(8,128)S(1)} collective-permute-done((f32[32,1408]{1,0:T(8,128)S(1)}, f32[32,1408]{1,0:T(8,128)S(1)}, u32[]{:S(2)}, u32[]{:S(2)}) %collective-permute-start.36) | collective-permute-done | bytes 180256 | tf_op jit(solution)/shard_map/ppermute | solution.py:201
  183.1 2.3 collective-permute-done.37
  187.6 2.1 collective-permute-done.44
  211.4 2.1 collective-permute-done.46
  223.4 2.1 collective-permute-done.47
  235.3 2.1 collective-permute-done.48
  242.0 3.0 %collective-permute-done.42 = f32[32,1408]{1,0:T(8,128)S(1)} collective-permute-done((f32[32,1408]{1,0:T(8,128)S(1)}, f32[32,1408]{1,0:T(8,128)S(1)}, u32[]{:S(2)}, u32[]{:S(2)}) %collective-permute-start.42) | collective-permute-done | bytes 180256 | tf_op jit(solution)/shard_map/ppermute | solution.py:201
  245.8 3.5 %collective-permute-done.49 = f32[32,1536]{1,0:T(8,128)S(1)} collective-permute-done((f32[32,1536]{1,0:T(8,128)S(1)}, f32[32,1536]{1,0:T(8,128)S(1)}, u32[]{:S(2)}, u32[]{:S(2)}) %collective-permute-start.49) | collective-permute-done | bytes 196640 | tf_op jit(solution)/shard_map/ppermute | solution.py:201
  (272 shorter events, 119.3 us)
Async XLA Ops:
  20.4 32.0 %collective-permute-start.1 = (f32[320,512]{1,0:T(8,128)S(1)}, f32[320,512]{1,0:T(8,128)S(1)}, u32[]{:S(2)}, u32[]{:S(2)}) collective-permute-start(f32[320,512]{1,0:T(8,128)S(1)} %dynamic-slice_add_fusion), channel_id=1, source_target_pairs={{0,2},{1,3},{2,0},{3,1},{4,6},{5,7},{6,4},{7,5},{8,10},{9,11},{10,... | collective-permute-start | bytes 1966088 | tf_op jit(solution)/shard_map/ppermute | solution.py:162
  23.0 22.6 %collective-permute-start.3 = (f32[320,256]{1,0:T(8,128)S(1)}, f32[320,256]{1,0:T(8,128)S(1)}, u32[]{:S(2)}, u32[]{:S(2)}) collective-permute-start(f32[320,256]{1,0:T(8,128)S(1)} %dynamic-slice_add_fusion.2), channel_id=1, source_target_pairs={{0,2},{1,3},{2,0},{3,1},{4,6},{5,7},{6,4},{7,5},{8,10},{9,11},{10,... | collective-permute-start | bytes 983048 | tf_op jit(solution)/shard_map/ppermute | solution.py:162
  23.1 29.2 %collective-permute-start.5 = (f32[320,256]{1,0:T(8,128)S(1)}, f32[320,256]{1,0:T(8,128)S(1)}, u32[]{:S(2)}, u32[]{:S(2)}) collective-permute-start(f32[320,256]{1,0:T(8,128)S(1)} %dynamic-slice_add_fusion.1), channel_id=1, source_target_pairs={{0,2},{1,3},{2,0},{3,1},{4,6},{5,7},{6,4},{7,5},{8,10},{9,11},{10,... | collective-permute-start | bytes 983048 | tf_op jit(solution)/shard_map/ppermute | solution.py:162
  58.7 13.9 %collective-permute-start.7 = (f32[320,512]{1,0:T(8,128)S(1)}, f32[320,512]{1,0:T(8,128)S(1)}, u32[]{:S(2)}, u32[]{:S(2)}) collective-permute-start(f32[320,512]{1,0:T(8,128)S(1)} %get-tuple-element.18), channel_id=1, source_target_pairs={{0,1},{1,0},{2,3},{3,2},{4,5},{5,4},{6,7},{7,6},{8,9},{9,8},{10,11... | collective-permute-start | bytes 1966088 | tf_op jit(solution)/shard_map/ppermute | solution.py:162
  84.5 31.2 %collective-permute-start.17 = (f32[64,512]{1,0:T(8,128)}, f32[64,512]{1,0:T(8,128)}, u32[]{:S(2)}, u32[]{:S(2)}) collective-permute-start(f32[64,512]{1,0:T(8,128)} %constant_dynamic-slice_fusion.36), channel_id=1, source_target_pairs={{0,8},{4,12},{8,0},{12,4},{16,24},{20,28},{24,16},{28,20},{1,9},{5... | collective-permute-start | bytes 393224 | tf_op jit(solution)/shard_map/ppermute | solution.py:162
  115.7 19.5 %collective-permute-start.15 = (f32[512,512]{1,0:T(8,128)}, f32[512,512]{1,0:T(8,128)}, u32[]{:S(2)}, u32[]{:S(2)}) collective-permute-start(f32[512,512]{1,0:T(8,128)} %inverse_factor.1), channel_id=1, source_target_pairs={{0,1},{1,0},{2,3},{3,2},{4,5},{5,4},{6,7},{7,6},{8,9},{9,8},{10,11... | collective-permute-start | bytes 3145736 | tf_op jit(solution)/shard_map/ppermute | solution.py:162
  133.8 14.0 %collective-permute-start.21 = (f32[256,512]{1,0:T(8,128)S(1)}, f32[256,512]{1,0:T(8,128)S(1)}, u32[]{:S(2)}, u32[]{:S(2)}) collective-permute-start(f32[256,512]{1,0:T(8,128)S(1)} %constant_dynamic-update-slice_fusion.1), channel_id=1, source_target_pairs={{0,2},{1,3},{2,0},{3,1},{4,6},{5,7},{6,4},{7,5},{8,10},{9,11},{10,... | collective-permute-start | bytes 1572872 | tf_op jit(solution)/shard_map/ppermute | solution.py:162
  164.3 13.4 %collective-permute-start.43 = (f32[32,1536]{1,0:T(8,128)S(1)}, f32[32,1536]{1,0:T(8,128)S(1)}, u32[]{:S(2)}, u32[]{:S(2)}) collective-permute-start(f32[32,1536]{1,0:T(8,128)S(1)} %constant_dynamic-slice_fusion.2), channel_id=1, source_target_pairs={{0,8},{8,16},{16,24},{24,28},{28,20},{20,12},{12,4},{4,0},{1,9},{9... | collective-permute-start | bytes 589832 | tf_op jit(solution)/shard_map/ppermute | solution.py:201
  169.6 12.3 %collective-permute-start.30 = (f32[32,1408]{1,0:T(8,128)S(1)}, f32[32,1408]{1,0:T(8,128)S(1)}, u32[]{:S(2)}, u32[]{:S(2)}) collective-permute-start(f32[32,1408]{1,0:T(8,128)S(1)} %maximum_add_fusion.7), channel_id=1, source_target_pairs={{8,0},{16,8},{24,16},{28,24},{20,28},{12,20},{4,12},{0,4},{9,1},{1... | collective-permute-start | bytes 540680 | tf_op jit(solution)/shard_map/ppermute | solution.py:201
  174.3 11.1 %collective-permute-start.37 = (f32[32,1408]{1,0:T(8,128)S(1)}, f32[32,1408]{1,0:T(8,128)S(1)}, u32[]{:S(2)}, u32[]{:S(2)}) collective-permute-start(f32[32,1408]{1,0:T(8,128)S(1)} %dynamic-slice_add_fusion.27), channel_id=1, source_target_pairs={{0,8},{8,16},{16,24},{24,28},{28,20},{20,12},{12,4},{4,0},{1,9},{9... | collective-permute-start | bytes 540680 | tf_op jit(solution)/shard_map/ppermute | solution.py:201
  178.5 11.1 %collective-permute-start.44 = (f32[32,1536]{1,0:T(8,128)S(1)}, f32[32,1536]{1,0:T(8,128)S(1)}, u32[]{:S(2)}, u32[]{:S(2)}) collective-permute-start(f32[32,1536]{1,0:T(8,128)S(1)} %dynamic-slice_add_fusion.14), channel_id=1, source_target_pairs={{0,8},{8,16},{16,24},{24,28},{28,20},{20,12},{12,4},{4,0},{1,9},{9... | collective-permute-start | bytes 589832 | tf_op jit(solution)/shard_map/ppermute | solution.py:201
  181.9 11.9 %collective-permute-start.31 = (f32[32,1408]{1,0:T(8,128)S(1)}, f32[32,1408]{1,0:T(8,128)S(1)}, u32[]{:S(2)}, u32[]{:S(2)}) collective-permute-start(f32[32,1408]{1,0:T(8,128)S(1)} %maximum_add_fusion.8), channel_id=1, source_target_pairs={{8,0},{16,8},{24,16},{28,24},{20,28},{12,20},{4,12},{0,4},{9,1},{1... | collective-permute-start | bytes 540680 | tf_op jit(solution)/shard_map/ppermute | solution.py:201
  190.4 11.1 %collective-permute-start.45 = (f32[32,1536]{1,0:T(8,128)S(1)}, f32[32,1536]{1,0:T(8,128)S(1)}, u32[]{:S(2)}, u32[]{:S(2)}) collective-permute-start(f32[32,1536]{1,0:T(8,128)S(1)} %dynamic-slice_add_fusion.13), channel_id=1, source_target_pairs={{0,8},{8,16},{16,24},{24,28},{28,20},{20,12},{12,4},{4,0},{1,9},{9... | collective-permute-start | bytes 589832 | tf_op jit(solution)/shard_map/ppermute | solution.py:201
  194.0 11.8 %collective-permute-start.32 = (f32[32,1408]{1,0:T(8,128)S(1)}, f32[32,1408]{1,0:T(8,128)S(1)}, u32[]{:S(2)}, u32[]{:S(2)}) collective-permute-start(f32[32,1408]{1,0:T(8,128)S(1)} %maximum_add_fusion.9), channel_id=1, source_target_pairs={{8,0},{16,8},{24,16},{28,24},{20,28},{12,20},{4,12},{0,4},{9,1},{1... | collective-permute-start | bytes 540680 | tf_op jit(solution)/shard_map/ppermute | solution.py:201
  202.4 11.1 %collective-permute-start.46 = (f32[32,1536]{1,0:T(8,128)S(1)}, f32[32,1536]{1,0:T(8,128)S(1)}, u32[]{:S(2)}, u32[]{:S(2)}) collective-permute-start(f32[32,1536]{1,0:T(8,128)S(1)} %dynamic-slice_add_fusion.12), channel_id=1, source_target_pairs={{0,8},{8,16},{16,24},{24,28},{28,20},{20,12},{12,4},{4,0},{1,9},{9... | collective-permute-start | bytes 589832 | tf_op jit(solution)/shard_map/ppermute | solution.py:201
  205.9 11.8 %collective-permute-start.33 = (f32[32,1408]{1,0:T(8,128)S(1)}, f32[32,1408]{1,0:T(8,128)S(1)}, u32[]{:S(2)}, u32[]{:S(2)}) collective-permute-start(f32[32,1408]{1,0:T(8,128)S(1)} %maximum_add_fusion.10), channel_id=1, source_target_pairs={{8,0},{16,8},{24,16},{28,24},{20,28},{12,20},{4,12},{0,4},{9,1},{1... | collective-permute-start | bytes 540680 | tf_op jit(solution)/shard_map/ppermute | solution.py:201
  210.2 11.1 %collective-permute-start.40 = (f32[32,1408]{1,0:T(8,128)S(1)}, f32[32,1408]{1,0:T(8,128)S(1)}, u32[]{:S(2)}, u32[]{:S(2)}) collective-permute-start(f32[32,1408]{1,0:T(8,128)S(1)} %dynamic-slice_add_fusion.24), channel_id=1, source_target_pairs={{0,8},{8,16},{16,24},{24,28},{28,20},{20,12},{12,4},{4,0},{1,9},{9... | collective-permute-start | bytes 540680 | tf_op jit(solution)/shard_map/ppermute | solution.py:201
  214.3 11.1 %collective-permute-start.47 = (f32[32,1536]{1,0:T(8,128)S(1)}, f32[32,1536]{1,0:T(8,128)S(1)}, u32[]{:S(2)}, u32[]{:S(2)}) collective-permute-start(f32[32,1536]{1,0:T(8,128)S(1)} %dynamic-slice_add_fusion.11), channel_id=1, source_target_pairs={{0,8},{8,16},{16,24},{24,28},{28,20},{20,12},{12,4},{4,0},{1,9},{9... | collective-permute-start | bytes 589832 | tf_op jit(solution)/shard_map/ppermute | solution.py:201
  217.8 11.8 %collective-permute-start.34 = (f32[32,1408]{1,0:T(8,128)S(1)}, f32[32,1408]{1,0:T(8,128)S(1)}, u32[]{:S(2)}, u32[]{:S(2)}) collective-permute-start(f32[32,1408]{1,0:T(8,128)S(1)} %maximum_add_fusion.11), channel_id=1, source_target_pairs={{8,0},{16,8},{24,16},{28,24},{20,28},{12,20},{4,12},{0,4},{9,1},{1... | collective-permute-start | bytes 540680 | tf_op jit(solution)/shard_map/ppermute | solution.py:201
  226.2 11.1 %collective-permute-start.48 = (f32[32,1536]{1,0:T(8,128)S(1)}, f32[32,1536]{1,0:T(8,128)S(1)}, u32[]{:S(2)}, u32[]{:S(2)}) collective-permute-start(f32[32,1536]{1,0:T(8,128)S(1)} %dynamic-slice_add_fusion.10), channel_id=1, source_target_pairs={{0,8},{8,16},{16,24},{24,28},{28,20},{20,12},{12,4},{4,0},{1,9},{9... | collective-permute-start | bytes 589832 | tf_op jit(solution)/shard_map/ppermute | solution.py:201
  229.8 15.3 %collective-permute-start.35 = (f32[32,1408]{1,0:T(8,128)S(1)}, f32[32,1408]{1,0:T(8,128)S(1)}, u32[]{:S(2)}, u32[]{:S(2)}) collective-permute-start(f32[32,1408]{1,0:T(8,128)S(1)} %maximum_add_fusion.12), channel_id=1, source_target_pairs={{8,0},{16,8},{24,16},{28,24},{20,28},{12,20},{4,12},{0,4},{9,1},{1... | collective-permute-start | bytes 540680 | tf_op jit(solution)/shard_map/ppermute | solution.py:201
  234.0 11.1 %collective-permute-start.42 = (f32[32,1408]{1,0:T(8,128)S(1)}, f32[32,1408]{1,0:T(8,128)S(1)}, u32[]{:S(2)}, u32[]{:S(2)}) collective-permute-start(f32[32,1408]{1,0:T(8,128)S(1)} %dynamic-slice_add_fusion.22), channel_id=1, source_target_pairs={{0,8},{8,16},{16,24},{24,28},{28,20},{20,12},{12,4},{4,0},{1,9},{9... | collective-permute-start | bytes 540680 | tf_op jit(solution)/shard_map/ppermute | solution.py:201
  237.4 12.0 %collective-permute-start.56 = (f32[32,1408]{1,0:T(8,128)S(1)}, f32[32,1408]{1,0:T(8,128)S(1)}, u32[]{:S(2)}, u32[]{:S(2)}) collective-permute-start(f32[32,1408]{1,0:T(8,128)S(1)} %dynamic-slice_add_fusion.16), channel_id=1, source_target_pairs={{8,0},{16,8},{24,16},{28,24},{20,28},{12,20},{4,12},{0,4},{9,1},{1... | collective-permute-start | bytes 540680 | tf_op jit(solution)/shard_map/ppermute | solution.py:201
  238.2 11.1 %collective-permute-start.49 = (f32[32,1536]{1,0:T(8,128)S(1)}, f32[32,1536]{1,0:T(8,128)S(1)}, u32[]{:S(2)}, u32[]{:S(2)}) collective-permute-start(f32[32,1536]{1,0:T(8,128)S(1)} %dynamic-slice_add_fusion.9), channel_id=1, source_target_pairs={{0,8},{8,16},{16,24},{24,28},{28,20},{20,12},{12,4},{4,0},{1,9},{9... | collective-permute-start | bytes 589832 | tf_op jit(solution)/shard_map/ppermute | solution.py:201
  (63 other events, 412.0 us)
